TPU v7x, 32 devices: a whole 2x2x4 slice. The times are simulated.
32 devices in a mesh: px: 8 (over y, x, core), py: 4 (over z).
Axes of the slice: x: 2, y: 2, z: 4, core: 2. Of those that a mesh axis runs over, the one named last changes fastest.
Arguments:
- trial_block: float32 [8, 4, 2, 8, 8192], P('px', 'py'), may hold values from -12 to 12
- stiff_coef: float32 [8, 4, 1024], P('px', 'py'), may hold values from 0.3 to 3
- mass_coef: float32 [8, 4, 1024], P('px', 'py'), may hold values from 1 to 12
- elem_count: int32 [8, 4], P('px', 'py'), may hold values from 256 to 1024, as said below
- elem_dofs: int32 [8, 4, 1024, 20], P('px', 'py'), may hold values from 0 to 12287, as said below
- pairing: int32 [2048], replicated, may hold values from 0 to 2047, each once
- bloch_fraction: int32 [2], replicated, may hold values from 1 to 16, as said below
- stiff_ref: float32 [20, 20], replicated, may hold values from -16 to 17, as said below
- mass_ref: float32 [20, 20], replicated, may hold values from -16 to 17, as said below
Outputs:
- curl_image: float32 [8, 4, 2, 8, 8192], P('px', 'py')
- mass_image: float32 [8, 4, 2, 8, 8192], P('px', 'py')
- gram: float32 [2, 2, 8, 8], replicated
Inputs may be any that keep to these rules, and one draw needn't show every extreme that they name: `elem_count`: element slots below 128 are the only ones that name indices of 8192 or more; each part's count is at least 256, and each part of a 2-by-2 block of parts has exactly 1024 in every draw. `elem_dofs`: indices into the extended layout; slots at or above 128 name only indices below 8192. bloch_fraction[1] is 16 and 0 < bloch_fraction[0] < bloch_fraction[1]. `stiff_ref`: symmetric positive definite. `mass_ref`: symmetric positive definite.
All inputs are finite; a program needn't handle non-finite values.
Results may differ from a plain program's by a relative error of at most 0.0003.
Values sent between devices are 32-bit elements; how exact they have to be, the bound alone decides.
No kernel may reach another device: no remote copies, remote signals or barrier semaphores. Data moves between devices by JAX's collectives and lax.ppermute only.
A program may use at most 64 MiB of HBM per device.

v0:
```python
import functools
import math

import jax
import jax.numpy as jnp
from jax import lax
from jax.experimental import pallas as pl
from jax.experimental.pallas import tpu as pltpu
from jax.sharding import PartitionSpec as P

LANES = 128
BLOCK_ROWS = 16
SUB_ROWS = 8
STEP = 4
DEEP = 4
N_ACC = 4
F32 = jnp.float32
BF16 = jnp.bfloat16


def ring_route(axis, steps):
    count = lax.axis_size(axis)
    return [(source, (source + steps) % count) for source in range(count)]


def line_route(axis, distance):
    devices = range(lax.axis_size(axis))
    return [(i - distance, i) for i in devices if i - distance in devices]


def iota(shape, axis):
    return lax.broadcasted_iota(jnp.int32, shape, axis)


def split(x):
    top = x.astype(BF16)
    return top, (x - top.astype(F32)).astype(BF16)


def dot_nt(left, right):
    return lax.dot_general(
        left, right, (((1,), (1,)), ((), ())), preferred_element_type=F32
    )


def gather_lanes(table_ref, index):
    high = index // LANES
    low = index % LANES
    found = jnp.zeros_like(index)
    for r in range(table_ref.shape[0]):
        line = jnp.broadcast_to(table_ref[r : r + 1, :], index.shape)
        found = jnp.where(high == r, jnp.take_along_axis(line, low, axis=1), found)
    return found


def prepare_kernel(
    owned_len, face_len, width, count_ref, bloch_ref,
    dofs_ref, pair_ref, stiff_ref, mass_ref,
    table_ref, own_table_ref, face_table_ref, scale_ref, turn_ref,
):
    nloc, _, capacity = dofs_ref.shape
    face_slots = face_table_ref.shape[1]
    groups = LANES // (2 * width)
    at_end = lax.axis_index("px") == lax.axis_size("px") - 1
    live = count_ref[0]

    index = [dofs_ref[i] for i in range(nloc)]
    flag = jnp.zeros((1, capacity), jnp.int32)
    for i in range(nloc):
        for k in range(i + 1, min(i // STEP * STEP + STEP, nloc)):
            flag = jnp.where(index[i] == index[k], 1, flag)
    reach = groups * SUB_ROWS // 2
    while reach:
        flag = jnp.maximum(flag, pltpu.roll(flag, reach, 1))
        reach //= 2
    table_ref[nloc] = flag
    own_table_ref[nloc] = flag
    for i in range(nloc):
        table_ref[i] = index[i]
        own_table_ref[i] = jnp.minimum(index[i], owned_len)

    pad = face_table_ref.shape[0] - nloc
    for c in range(0, face_slots, LANES):
        at = slice(c, c + LANES)
        first = jnp.concatenate(
            [row[:, at] for row in index] + [jnp.zeros((pad, LANES), jnp.int32)], axis=0
        )
        local = first - owned_len
        on_face = at_end & (local >= 0) & (local < face_len)
        paired = gather_lanes(pair_ref, jnp.where(on_face, local, 0))
        first = jnp.where(on_face, paired + owned_len, first)
        face_table_ref[:, at] = jnp.where(first >= owned_len, first - owned_len, 2 * face_len)
        for i in range(nloc):
            table_ref[i, :, at] = first[i : i + 1]

    per_chunk = LANES // groups
    lane_of = iota((LANES, LANES), 0)
    elem_of = iota((LANES, LANES), 1)
    mine = elem_of % groups == lane_of // (2 * width)
    is_curl = lane_of // width % 2 == 0
    chooser = (iota((per_chunk, LANES), 1) // groups == iota((per_chunk, LANES), 0)).astype(BF16)
    chooser = jnp.concatenate([chooser, chooser], axis=1)
    for c in range(capacity // LANES):
        at = slice(c * LANES, (c + 1) * LANES)
        scales = jnp.where(is_curl, stiff_ref[:, at], mass_ref[:, at])
        scales = jnp.where(mine & (c * LANES + elem_of < live), scales, 0.0)
        scale_ref[c * per_chunk : (c + 1) * per_chunk, :] = dot_nt(
            chooser, jnp.concatenate(split(scales), axis=1)
        )

    ratio = jnp.full((8, LANES), bloch_ref[0].astype(F32), F32) / bloch_ref[1].astype(F32)
    angle = (2.0 * math.pi) * jnp.where(at_end, ratio, 0.0)
    turn_ref[:8] = jnp.cos(angle)
    turn_ref[8:] = jnp.sin(angle)


def lane_masks(width, groups):
    lane = iota((1, LANES), 1) // (2 * width)
    return [lane == k for k in range(groups)]


def pick(masks, parts):
    out = parts[-1]
    for mask, part in zip(masks[-2::-1], parts[-2::-1]):
        out = jnp.where(mask, part, out)
    return out


def folder_of(width):
    rows = 2 * width
    folder = (iota((rows, LANES), 1) % rows == iota((rows, LANES), 0)).astype(BF16)
    return jnp.concatenate([folder, folder], axis=1)


def add_block(term_ref, accs, index_of, b, nloc, groups):
    unroll = 2

    def run(step, first_row, first_elem):
        def some(t, c):
            for u in range(unroll):
                g = t * unroll + u
                elem = first_elem + g * groups
                for j in range(0, nloc, step):
                    slots = range(j, min(j + step, nloc))
                    new = [term_ref[pl.ds(first_row + s * BLOCK_ROWS + g, 1), :] for s in slots]
                    for k in range(groups):
                        places = [pl.ds(index_of[0](s, elem + k), 1) for s in slots]
                        sums = [accs[k][at, :] + row for at, row in zip(places, new)]
                        for at, row in zip(places, sums):
                            accs[k][at, :] = row
            return c

        lax.fori_loop(0, SUB_ROWS // unroll, some, 0)

    def part(h, carry):
        first_row = b * nloc * BLOCK_ROWS + h * SUB_ROWS
        first_elem = (b * (BLOCK_ROWS // SUB_ROWS) + h) * SUB_ROWS * groups
        clash = index_of[1](nloc, first_elem + SUB_ROWS * groups - 1)

        @pl.when(clash == 0)
        def _():
            run(STEP, first_row, first_elem)

        @pl.when(clash != 0)
        def _():
            run(1, first_row, first_elem)

        return carry

    index_of = index_of if isinstance(index_of, tuple) else (index_of, index_of)
    lax.fori_loop(0, BLOCK_ROWS // SUB_ROWS, part, 0)


def term_kernel(
    width,
    count_ref,
    stiff_ref,
    mass_ref,
    table_hbm,
    face_table_hbm,
    turn_ref,
    own_ref,
    high_x_ref,
    high_y_ref,
    scale_ref,
    term_hbm,
    side_x_ref,
    side_y_ref,
    gram_ref,
    dofs_ref,
    face_dofs_ref,
    term_ref,
    coef_ref,
    rows_x,
    gath,
    gram_acc,
    sems,
    term_sems,
    *accs,
):
    owned_len = own_ref.shape[1]
    face_len = high_x_ref.shape[1]
    vecs = width // 2
    groups = LANES // (2 * width)
    capacity = scale_ref.shape[0] * groups
    nloc = stiff_ref.shape[0]
    face_slots = capacity // 8
    copies = LANES // width
    block_elems = groups * BLOCK_ROWS
    block_terms = nloc * BLOCK_ROWS

    loads = [
        pltpu.make_async_copy(table_hbm, dofs_ref, sems.at[0]),
        pltpu.make_async_copy(face_table_hbm, face_dofs_ref, sems.at[1]),
    ]
    for load in loads:
        load.start()

    cos, sin = turn_ref[:vecs], turn_ref[8 : 8 + vecs]

    def turned(pair, sign):
        n = pair.shape[1] // LANES
        c = jnp.concatenate([cos] * n, axis=1)
        s = jnp.concatenate([sin] * n, axis=1) * sign
        a, b = pair[:vecs], pair[vecs:]
        return jnp.concatenate([c * a - s * b, s * a + c * b], axis=0)

    unit = (iota((LANES, LANES), 0) == iota((LANES, LANES), 1)).astype(BF16)
    unit = jnp.concatenate([unit, unit], axis=1)
    zero_tile = jnp.zeros((LANES, LANES), F32)

    def put_rows(tile, first):
        top, low = split(tile)
        tiled = jnp.concatenate(
            [jnp.concatenate([top] * copies, axis=0), jnp.concatenate([low] * copies, axis=0)],
            axis=1,
        )
        rows_x[pl.ds(first, LANES), :] = dot_nt(unit, tiled)

    many = 8

    def build_own(c, carry):
        for u in range(many):
            first = pl.multiple_of((c * many + u) * LANES, LANES)
            put_rows(own_ref[:, pl.ds(first, LANES)], first)
        return carry

    lax.fori_loop(0, owned_len // (many * LANES), build_own, 0)

    def build_face(c, carry):
        for u in range(many // 2):
            first = pl.multiple_of((c * (many // 2) + u) * LANES, LANES)
            put_rows(
                turned(high_x_ref[:, pl.ds(first, LANES)], 1.0),
                pl.multiple_of(owned_len + first, LANES),
            )
            put_rows(
                high_y_ref[:, pl.ds(first, LANES)],
                pl.multiple_of(owned_len + face_len + first, LANES),
            )
            for acc in accs:
                acc[pl.ds(pl.multiple_of(2 * first, 2 * LANES), LANES), :] = zero_tile
                acc[pl.ds(pl.multiple_of(2 * first + LANES, LANES), LANES), :] = zero_tile
        return carry

    lax.fori_loop(0, face_len // (many // 2 * LANES), build_face, 0)

    curl_lane = iota((8, LANES), 1) // width % 2 == 0

    def build_coef(j, carry):
        for i in range(nloc):
            coef_ref[j * nloc + i] = jnp.where(curl_lane, stiff_ref[j, i], mass_ref[j, i])
        return carry

    lax.fori_loop(0, nloc, build_coef, 0)
    gram_acc[...] = jnp.zeros_like(gram_acc)

    for load in loads:
        load.wait()

    masks = lane_masks(width, groups)

    def index_of(i, elem):
        return dofs_ref.at[pl.ds(i * capacity, capacity)][elem]

    def face_index_of(i, elem):
        return face_dofs_ref.at[pl.ds(i * face_slots, face_slots)][elem]

    unroll = 4
    steps = BLOCK_ROWS // unroll
    halves = range(0, BLOCK_ROWS, 8)
    part = nloc // steps

    def block(b, gather):
        behind = jnp.maximum(b - 1, 0)
        here = pl.multiple_of(b * block_terms, BLOCK_ROWS)
        there = pl.multiple_of(behind * block_terms, BLOCK_ROWS)
        first_term = pl.multiple_of(behind * block_terms, BLOCK_ROWS)
        first_elem = b * block_elems

        def step(t, c):
            totals = [[None] * len(halves) for _ in range(part)]
            for i in range(nloc):
                if gather:
                    for u in range(unroll):
                        g = t * unroll + u
                        elem = first_elem + g * groups
                        rows = [
                            rows_x[pl.ds(index_of(i, elem + k), 1), :] for k in range(groups)
                        ]
                        gath[pl.ds(here + i * BLOCK_ROWS + g, 1), :] = pick(masks, rows)
                values = [
                    gath[pl.ds(pl.multiple_of(there + i * BLOCK_ROWS + h, 8), 8), :] for h in halves
                ]
                for q in range(part):
                    coef = coef_ref[(t * part + q) * nloc + i]
                    for n, value in enumerate(values):
                        product = coef * value
                        totals[q][n] = product if i == 0 else totals[q][n] + product
            for n, h in enumerate(halves):
                scale = scale_ref[pl.ds(pl.multiple_of(behind * BLOCK_ROWS + h, 8), 8), :]
                for q in range(part):
                    at = first_term + (t * part + q) * BLOCK_ROWS + h
                    term_ref[pl.ds(pl.multiple_of(at, 8), 8), :] = totals[q][n] * scale
            return c

        lax.fori_loop(0, steps, step, 0)

    def send(b):
        at = pl.ds(pl.multiple_of(b * block_terms, BLOCK_ROWS), block_terms)
        return pltpu.make_async_copy(term_ref.at[at], term_hbm.at[at], term_sems.at[b])

    def face_block(b, carry):
        add_block(term_ref, accs, (face_index_of, index_of), b, nloc, groups)
        return carry

    live = count_ref[0]
    blocks = (live + block_elems - 1) // block_elems
    face_blocks = jnp.minimum(blocks, face_slots // block_elems)
    def full_block(b, carry):
        block(b, True)

        @pl.when(b > 0)
        def _():
            send(b - 1).start()

        return carry

    lax.fori_loop(0, blocks, full_block, 0)
    block(blocks, False)
    send(blocks - 1).start()
    lax.fori_loop(0, face_blocks, face_block, 0)

    deep = DEEP * block_terms
    zero_block = jnp.zeros((block_terms, LANES), F32)
    chunks = (blocks + DEEP - 1) // DEEP

    def blank(b, carry):
        at = pl.ds(pl.multiple_of(b * block_terms, BLOCK_ROWS), block_terms)
        gath[at, :] = zero_block
        term_ref[at, :] = zero_block
        return carry

    lax.fori_loop(blocks, chunks * DEEP, blank, 0)

    def products(c, carry):
        at = pl.ds(pl.multiple_of(c * deep, BLOCK_ROWS), deep)
        left, left_low = split(gath[at, :])
        right, right_low = split(term_ref[at, :])
        gram_acc[...] += lax.dot_general(
            jnp.concatenate([left, left, left_low], axis=0),
            jnp.concatenate([right, right_low, right], axis=0),
            (((0,), (0,)), ((), ())),
            preferred_element_type=F32,
        )
        return carry

    lax.fori_loop(0, chunks, products, 0)
    folder = folder_of(width)
    wide = 2 * LANES

    def folded(first):
        at = pl.ds(first, wide)
        total = pick(masks, [acc[at, :] for acc in accs])
        return dot_nt(folder, jnp.concatenate(split(total), axis=1))

    def fold_face(c, carry):
        for u in range(2):
            first = pl.multiple_of((2 * c + u) * wide, wide)
            at = pl.ds(first, wide)
            total = folded(first)
            side_x_ref[:width, at] = turned(total[:width], -1.0)
            side_x_ref[width:, at] = turned(total[width:], -1.0)
            side_y_ref[:, at] = folded(pl.multiple_of(face_len + first, wide))
        return carry

    lax.fori_loop(0, face_len // (2 * wide), fold_face, 0)

    whole = gram_acc[...]
    total = whole[:width]
    for k in range(1, groups):
        part = whole[2 * width * k : 2 * width * k + width]
        total = total + pltpu.roll(part, LANES - 2 * width * k, 1)
    re_left, im_left = total[:vecs], total[vecs:]
    lane = iota((vecs, LANES), 1)
    real_here = lane // vecs % 2 == 0
    swapped = jnp.where(
        real_here, pltpu.roll(im_left, LANES - vecs, 1), -pltpu.roll(im_left, vecs, 1)
    )
    joined = re_left + swapped
    for n in range(gram_ref.shape[0]):
        gram_ref[n] = joined

    def sent(b, carry):
        send(b).wait()
        return carry

    lax.fori_loop(0, blocks, sent, 0)


def add_kernel(
    width, nloc, interior, count_ref, table_hbm, term_hbm, curl_hbm, mass_hbm, face_ref,
    dofs_ref, term_ref, images, sem, term_sems, out_sems, *accs
):
    owned_len = curl_hbm.shape[1]
    groups = LANES // (2 * width)
    capacity = term_ref.shape[0] // nloc * groups
    block_elems = groups * BLOCK_ROWS
    block_terms = nloc * BLOCK_ROWS
    load = pltpu.make_async_copy(table_hbm, dofs_ref, sem)
    load.start()
    live = count_ref[0]
    blocks = (live + block_elems - 1) // block_elems

    def fetch(b):
        at = pl.ds(pl.multiple_of(b * block_terms, BLOCK_ROWS), block_terms)
        return pltpu.make_async_copy(term_hbm.at[at], term_ref.at[at], term_sems.at[b])

    def fetch_all(b, carry):
        fetch(b).start()
        return carry

    lax.fori_loop(0, blocks, fetch_all, 0)
    many = 4
    zero_tile = jnp.zeros((many * LANES, LANES), F32)

    def clear(c, carry):
        at = pl.ds(pl.multiple_of(c * many * LANES, LANES), many * LANES)
        for acc in accs:
            acc[at, :] = zero_tile
        return carry

    lax.fori_loop(0, owned_len // (many * LANES), clear, 0)
    load.wait()

    def index_of(i, elem):
        return dofs_ref.at[pl.ds(i * capacity, capacity)][elem]

    def block(b, carry):
        fetch(b).wait()
        add_block(term_ref, accs, index_of, b, nloc, groups)
        return carry

    lax.fori_loop(0, blocks, block, 0)

    masks = lane_masks(width, groups)
    folder = folder_of(width)
    wide = 2 * LANES
    many = 4
    span = many * wide

    def fold_some(first, curl, mass):
        for u in range(many):
            at = pl.ds(pl.multiple_of(first + u * wide, wide), wide)
            total = pick(masks, [acc[at, :] for acc in accs])
            total = dot_nt(folder, jnp.concatenate(split(total), axis=1))
            to = slice(u * wide, (u + 1) * wide)
            curl[:, to] = total[:width]
            mass[:, to] = total[width:]

    moves = []
    for c in range(owned_len // span):
        at = pl.ds(c * span, span)
        if c * span < interior:
            fold_some(c * span, images.at[0, :, at], images.at[1, :, at])
            for n, image in enumerate((curl_hbm, mass_hbm)):
                moves.append(
                    pltpu.make_async_copy(
                        images.at[n, :, at], image.at[:, at], out_sems.at[2 * c + n]
                    )
                )
                moves[-1].start()
        else:
            at = pl.ds(c * span - interior, span)
            fold_some(c * span, face_ref.at[0, :, at], face_ref.at[1, :, at])
    for move in moves:
        move.wait()


def finish_kernel(
    width, scale, curl_in, mass_in, face_ref, back_x_ref, back_y_ref, gram_ref,
    curl_out, mass_out, gram_out, faces, sems,
):
    del curl_in, mass_in
    face_len = back_x_ref.shape[1]
    outer = pl.ds(curl_out.shape[1] - 2 * face_len, 2 * face_len)
    moves = []
    for n, image in enumerate((curl_out, mass_out)):
        rows = slice(n * width, (n + 1) * width)
        faces[n, :, :face_len] = face_ref[n, :, :face_len] + back_x_ref[rows, :]
        faces[n, :, face_len:] = face_ref[n, :, face_len:] + back_y_ref[rows, :]
        moves.append(pltpu.make_async_copy(faces.at[n], image.at[:, outer], sems.at[n]))
        moves[-1].start()
    total = gram_ref[0]
    for d in range(1, gram_ref.shape[0]):
        total = total + gram_ref[d]
    total = total * scale
    vecs = total.shape[0]
    for q in range(4):
        shifted = total if q == 0 else pltpu.roll(total, LANES - q * vecs, 1)
        gram_out[q * vecs : (q + 1) * vecs, :] = shifted[:, :vecs]
    for move in moves:
        move.wait()


def on_device(
    trial_block,
    stiff_coef,
    mass_coef,
    elem_count,
    elem_dofs,
    pairing,
    bloch_fraction,
    stiff_ref,
    mass_ref,
):
    own_block = trial_block[0, 0]
    vecs, owned_len = own_block.shape[1:]
    face_len = pairing.shape[0]
    interior = owned_len - 2 * face_len
    width = 2 * vecs
    groups = LANES // (2 * width)
    capacity, nloc = elem_dofs.shape[2:]
    face_slots = capacity // 8
    devices = lax.axis_size("px") * lax.axis_size("py")
    own_rows = own_block.reshape(width, owned_len)
    low_x = own_rows[:, interior : interior + face_len]
    low_y = own_rows[:, interior + face_len :]
    high_x = lax.ppermute(low_x, "px", ring_route("px", -1))
    high_y = lax.ppermute(low_y, "py", line_route("py", -1))
    live = elem_count[0]
    smem = pl.BlockSpec(memory_space=pltpu.SMEM)
    vmem = pl.BlockSpec(memory_space=pltpu.VMEM)
    left = pl.BlockSpec(memory_space=pl.ANY)

    limit = 62 * 1024 * 1024
    params = pltpu.CompilerParams(vmem_limit_bytes=limit)
    table, own_table, face_table, scale, turn = pl.pallas_call(
        functools.partial(prepare_kernel, owned_len, face_len, width),
        out_shape=(
            jax.ShapeDtypeStruct((nloc + 1, 1, capacity), jnp.int32),
            jax.ShapeDtypeStruct((nloc + 1, 1, capacity), jnp.int32),
            jax.ShapeDtypeStruct((-(-nloc // 8) * 8, face_slots), jnp.int32),
            jax.ShapeDtypeStruct((capacity // groups, LANES), F32),
            jax.ShapeDtypeStruct((16, LANES), F32),
        ),
        in_specs=[smem] * 2 + [vmem] * 4,
        out_specs=[vmem] * 5,
        compiler_params=params,
        name="prepare",
    )(
        live,
        bloch_fraction,
        elem_dofs.transpose(0, 3, 1, 2).reshape(nloc, 1, capacity),
        pairing.reshape(-1, LANES),
        stiff_coef[0],
        mass_coef[0],
    )
    table = table.reshape(-1)
    own_table = own_table.reshape(-1)
    face_table = face_table.reshape(-1)

    extent = owned_len + 2 * face_len
    blocks = capacity // (groups * BLOCK_ROWS)
    term_rows = nloc * capacity // groups
    terms, side_x, side_y, gram = pl.pallas_call(
        functools.partial(term_kernel, width),
        out_shape=(
            jax.ShapeDtypeStruct((term_rows, LANES), F32),
            jax.ShapeDtypeStruct((2 * width, face_len), F32),
            jax.ShapeDtypeStruct((2 * width, face_len), F32),
            jax.ShapeDtypeStruct((devices, vecs, LANES), F32),
        ),
        in_specs=[smem] * 3 + [left] * 2 + [vmem] * 5,
        out_specs=[left] + [vmem] * 3,
        scratch_shapes=[
            pltpu.SMEM(table.shape, jnp.int32),
            pltpu.SMEM(face_table.shape, jnp.int32),
            pltpu.VMEM((term_rows, LANES), F32),
            pltpu.VMEM((nloc * nloc, 8, LANES), F32),
            pltpu.VMEM((extent, LANES), F32),
            pltpu.VMEM((term_rows, LANES), F32),
            pltpu.VMEM((LANES, LANES), F32),
            pltpu.SemaphoreType.DMA((2,)),
            pltpu.SemaphoreType.DMA((blocks,)),
        ]
        + [pltpu.VMEM((2 * face_len + 8, LANES), F32)] * N_ACC,
        compiler_params=pltpu.CompilerParams(vmem_limit_bytes=60 * 1024 * 1024),
        name="terms",
    )(
        live, stiff_ref, mass_ref, table, face_table, turn, own_rows, high_x, high_y, scale
    )

    gathered = lax.all_to_all(gram, ("px", "py"), 0, 0)
    back_x = lax.ppermute(side_x, "px", ring_route("px", 1))
    back_y = lax.ppermute(side_y, "py", line_route("py", 1))

    curl, mass, faces = pl.pallas_call(
        functools.partial(add_kernel, width, nloc, interior),
        out_shape=(
            jax.ShapeDtypeStruct((width, owned_len), F32),
            jax.ShapeDtypeStruct((width, owned_len), F32),
            jax.ShapeDtypeStruct((2, width, 2 * face_len), F32),
        ),
        in_specs=[smem, left, left],
        out_specs=[left, left, vmem],
        scratch_shapes=[
            pltpu.SMEM(own_table.shape, jnp.int32),
            pltpu.VMEM((term_rows, LANES), F32),
            pltpu.VMEM((2, width, interior), F32),
            pltpu.SemaphoreType.DMA,
            pltpu.SemaphoreType.DMA((blocks,)),
            pltpu.SemaphoreType.DMA((2 * owned_len // (8 * LANES),)),
        ]
        + [pltpu.VMEM((owned_len + 8, LANES), F32)] * N_ACC,
        compiler_params=params,
        cost_estimate=pl.CostEstimate(
            flops=40 * 1024 * 1024 * 1024, bytes_accessed=40 * 1024 * 1024, transcendentals=0
        ),
        name="adds",
    )(live, own_table, terms)

    curl, mass, gram = pl.pallas_call(
        functools.partial(finish_kernel, width, 1.0 / float(devices * owned_len)),
        out_shape=(
            jax.ShapeDtypeStruct((width, owned_len), F32),
            jax.ShapeDtypeStruct((width, owned_len), F32),
            jax.ShapeDtypeStruct((4 * vecs, vecs), F32),
        ),
        in_specs=[left] * 2 + [vmem] * 4,
        out_specs=[left, left, vmem],
        scratch_shapes=[
            pltpu.VMEM((2, width, 2 * face_len), F32),
            pltpu.SemaphoreType.DMA((2,)),
        ],
        input_output_aliases={0: 0, 1: 1},
        compiler_params=pltpu.CompilerParams(vmem_limit_bytes=8 * 1024 * 1024),
        name="finish",
    )(curl, mass, faces, back_x, back_y, gathered)
    shape = (1, 1, 2, vecs, owned_len)
    return curl.reshape(shape), mass.reshape(shape), gram.reshape(2, 2, vecs, vecs)


def solution(mesh):
    return jax.shard_map(
        on_device,
        mesh=mesh,
        in_specs=(
            P("px", "py", None, None, None),
            P("px", "py", None),
            P("px", "py", None),
            P("px", "py"),
            P("px", "py", None, None),
            P(),
            P(),
            P(),
            P(),
        ),
        out_specs=(P("px", "py", None, None, None), P("px", "py", None, None, None), P()),
        check_vma=False,
    )
```

profile of v0, /device:TPU:17, one launch (start us, length us, event | category | flops | bytes accessed | tf_op | source)
XLA Modules:
  0.0 68.2 jit_solution(11909916770892208697)
XLA Ops:
  0.6 1.0 %fusion = (f32[16,2048]{1,0:T(8,128)S(1)}, f32[16,2048]{1,0:T(8,128)S(1)}) fusion(f32[16,8192]{1,0:T(8,128)} %bitcast.17), kind=kLoop, calls=%fused_computation | loop fusion | bytes 524288 | tf_op jit(solution)/shard_map/slice | solution.py:548
  1.6 2.1 %collective-permute-start.1 = (f32[16,2048]{1,0:T(8,128)S(1)}, f32[16,2048]{1,0:T(8,128)S(1)}, u32[]{:S(2)}, u32[]{:S(2)}) collective-permute-start(f32[16,2048]{1,0:T(8,128)S(1)} %get-tuple-element.33), channel_id=1, source_target_pairs={{1,0},{2,1},{3,2},{5,4},{6,5},{7,6},{9,8},{10,9},{11,10},{13,12},{... | collective-permute-start | bytes 393224 | tf_op jit(solution)/shard_map/ppermute | solution.py:550
  3.7 1.0 %collective-permute-start = (f32[16,2048]{1,0:T(8,128)S(1)}, f32[16,2048]{1,0:T(8,128)S(1)}, u32[]{:S(2)}, u32[]{:S(2)}) collective-permute-start(f32[16,2048]{1,0:T(8,128)S(1)} %get-tuple-element.34), channel_id=1, source_target_pairs={{0,28},{4,0},{8,4},{12,8},{16,12},{20,16},{24,20},{28,24},{1,29},{... | collective-permute-start | bytes 393224 | tf_op jit(solution)/shard_map/ppermute | solution.py:549
  5.4 2.1 %prepare.1 = (s32[21,1,1024]{2,1,0:T(1,128)}, s32[21,1,1024]{2,1,0:T(1,128)}, s32[24,128]{1,0:T(8,128)}, f32[256,128]{1,0:T(8,128)}, f32[16,128]{1,0:T(8,128)}) custom-call(s32[1]{0:T(128)} %bitcast.14.count_ref, s32[2]{0:T(128)} %bloch_ref.1, s32[20,1,1024]{2,1,0:T(1,128)} %bitcast.22, s32[16,128]{1,0:T(8,128)} %bitcast.24, f32[1,1024]{1,0:T(1,128)} %bitcast.25, ...), custom_call_target="tpu_custom_call" | custom-call | tf_op jit(solution)/shard_map/prepare/pallas_call | solution.py:558
  7.4 0.5 collective-permute-done.1.high_y_ref
  7.9 0.0 copy-start.1
  7.9 0.9 %collective-permute-done.high_x_ref = f32[16,2048]{1,0:T(8,128)S(1)} collective-permute-done((f32[16,2048]{1,0:T(8,128)S(1)}, f32[16,2048]{1,0:T(8,128)S(1)}, u32[]{:S(2)}, u32[]{:S(2)}) %collective-permute-start) | collective-permute-done | bytes 131104 | tf_op jit(solution)/shard_map/ppermute | solution.py:549
  8.8 0.0 copy-start.2
  8.8 0.0 copy-done.1
  8.8 0.7 copy-done.2
  9.4 28.3 %terms.1 = (f32[5120,128]{1,0:T(8,128)}, f32[32,2048]{1,0:T(8,128)}, f32[32,2048]{1,0:T(8,128)}, f32[32,8,128]{2,1,0:T(8,128)}) custom-call(s32[1]{0:T(128)} %bitcast.15.count_ref, f32[20,20]{1,0:T(8,128)} %stiff_ref.1, f32[20,20]{1,0:T(8,128)} %mass_ref.1, s32[21504]{0:T(1024)} %bitcast.21, s32[3072]{0:T(1024)} %bitcast.23, ...), custom_call_target="tpu_custom_call" | custom-call | tf_op jit(solution)/shard_map/terms/pallas_call | solution.py:586
  37.8 4.3 %all-to-all-start = ((f32[32,8,128]{2,1,0:T(8,128)}), f32[32,8,128]{2,1,0:T(8,128)S(1)}, u32[]{:S(2)}, u32[]{:S(2)}) async-start(f32[32,8,128]{2,1,0:T(8,128)} %get-tuple-element.29), calls=%async_computation | async-start | bytes 262144 | tf_op jit(solution)/shard_map/all_to_all | solution.py:614
  42.1 1.5 %collective-permute-start.2 = (f32[32,2048]{1,0:T(8,128)}, f32[32,2048]{1,0:T(8,128)S(1)}, u32[]{:S(2)}, u32[]{:S(2)}) collective-permute-start(f32[32,2048]{1,0:T(8,128)} %get-tuple-element.27), channel_id=1, source_target_pairs={{0,4},{4,8},{8,12},{12,16},{16,20},{20,24},{24,28},{28,0},{1,5},{5... | collective-permute-start | bytes 786440 | tf_op jit(solution)/shard_map/ppermute | solution.py:615
  43.6 3.1 %collective-permute-start.3 = (f32[32,2048]{1,0:T(8,128)}, f32[32,2048]{1,0:T(8,128)S(1)}, u32[]{:S(2)}, u32[]{:S(2)}) collective-permute-start(f32[32,2048]{1,0:T(8,128)} %get-tuple-element.28), channel_id=1, source_target_pairs={{0,1},{1,2},{2,3},{4,5},{5,6},{6,7},{8,9},{9,10},{10,11},{12,13},{... | collective-permute-start | bytes 786440 | tf_op jit(solution)/shard_map/ppermute | solution.py:616
  46.7 19.0 %adds.1 = (f32[16,8192]{1,0:T(8,128)}, f32[16,8192]{1,0:T(8,128)}, f32[2,16,4096]{2,1,0:T(8,128)}) custom-call(s32[1]{0:T(128)} %bitcast.16.count_ref, s32[21504]{0:T(1024)} %bitcast.27, f32[5120,128]{1,0:T(8,128)} %get-tuple-element.23.term_hbm), custom_call_target="tpu_custom_call" | custom-call | flops 42949672960 | bytes 41943040 | tf_op jit(solution)/shard_map/adds/pallas_call | solution.py:618
  65.7 0.0 all-to-all-done.gram_ref
  65.7 0.0 collective-permute-done.2.back_x_ref
  65.7 0.0 collective-permute-done.3.back_y_ref
  65.7 0.0 copy-start
  65.7 1.0 %copy-done = f32[2,16,4096]{2,1,0:T(8,128)S(1)} copy-done((f32[2,16,4096]{2,1,0:T(8,128)S(1)}, f32[2,16,4096]{2,1,0:T(8,128)}, u32[]{:S(2)}) %copy-start) | copy-done | bytes 524312
  66.8 1.5 %finish.1 = (f32[16,8192]{1,0:T(8,128)}, f32[16,8192]{1,0:T(8,128)}, f32[32,8]{1,0:T(8,128)}) custom-call(f32[16,8192]{1,0:T(8,128)} %get-tuple-element.24.curl_in, f32[16,8192]{1,0:T(8,128)} %get-tuple-element.25.mass_in, f32[2,16,4096]{2,1,0:T(8,128)S(1)} %copy-done, ...), custom_call_target="tpu_custom_call", output_to_operand_aliasing={{0}: (0, {}), {1}: (1, {})} | custom-call | tf_op jit(solution)/shard_map/finish/pallas_call | solution.py:643
Async XLA Ops:
  1.6 6.3 %collective-permute-start.1 = (f32[16,2048]{1,0:T(8,128)S(1)}, f32[16,2048]{1,0:T(8,128)S(1)}, u32[]{:S(2)}, u32[]{:S(2)}) collective-permute-start(f32[16,2048]{1,0:T(8,128)S(1)} %get-tuple-element.33), channel_id=1, source_target_pairs={{1,0},{2,1},{3,2},{5,4},{6,5},{7,6},{9,8},{10,9},{11,10},{13,12},{... | collective-permute-start | bytes 393224 | tf_op jit(solution)/shard_map/ppermute | solution.py:550
  3.7 5.1 %collective-permute-start = (f32[16,2048]{1,0:T(8,128)S(1)}, f32[16,2048]{1,0:T(8,128)S(1)}, u32[]{:S(2)}, u32[]{:S(2)}) collective-permute-start(f32[16,2048]{1,0:T(8,128)S(1)} %get-tuple-element.34), channel_id=1, source_target_pairs={{0,28},{4,0},{8,4},{12,8},{16,12},{20,16},{24,20},{28,24},{1,29},{... | collective-permute-start | bytes 393224 | tf_op jit(solution)/shard_map/ppermute | solution.py:549
  7.9 0.9 %copy-start.1 = (f32[16,2048]{1,0:T(8,128)}, f32[16,2048]{1,0:T(8,128)S(1)}, u32[]{:S(2)}) copy-start(f32[16,2048]{1,0:T(8,128)S(1)} %collective-permute-done.1.high_y_ref) | copy-start | bytes 393220
  8.8 0.7 copy-start.2
  37.8 27.9 %all-to-all-start = ((f32[32,8,128]{2,1,0:T(8,128)}), f32[32,8,128]{2,1,0:T(8,128)S(1)}, u32[]{:S(2)}, u32[]{:S(2)}) async-start(f32[32,8,128]{2,1,0:T(8,128)} %get-tuple-element.29), calls=%async_computation | async-start | bytes 262144 | tf_op jit(solution)/shard_map/all_to_all | solution.py:614
  42.1 23.7 %collective-permute-start.2 = (f32[32,2048]{1,0:T(8,128)}, f32[32,2048]{1,0:T(8,128)S(1)}, u32[]{:S(2)}, u32[]{:S(2)}) collective-permute-start(f32[32,2048]{1,0:T(8,128)} %get-tuple-element.27), channel_id=1, source_target_pairs={{0,4},{4,8},{8,12},{12,16},{16,20},{20,24},{24,28},{28,0},{1,5},{5... | collective-permute-start | bytes 786440 | tf_op jit(solution)/shard_map/ppermute | solution.py:615
  43.6 22.2 %collective-permute-start.3 = (f32[32,2048]{1,0:T(8,128)}, f32[32,2048]{1,0:T(8,128)S(1)}, u32[]{:S(2)}, u32[]{:S(2)}) collective-permute-start(f32[32,2048]{1,0:T(8,128)} %get-tuple-element.28), channel_id=1, source_target_pairs={{0,1},{1,2},{2,3},{4,5},{5,6},{6,7},{8,9},{9,10},{10,11},{12,13},{... | collective-permute-start | bytes 786440 | tf_op jit(solution)/shard_map/ppermute | solution.py:616
  65.7 1.0 %copy-start = (f32[2,16,4096]{2,1,0:T(8,128)S(1)}, f32[2,16,4096]{2,1,0:T(8,128)}, u32[]{:S(2)}) copy-start(f32[2,16,4096]{2,1,0:T(8,128)} %get-tuple-element.26.face_ref) | copy-start | bytes 1572868
where the time goes:
time: 69.2 us; the launch traced here: 68.2 us
  Pallas kernels  50.8 us (73%)
  starting transfers between devices  12 us (17%)
  local copies, waits for them, and re-layouts  2.68 us (4%)
  between operations  1.36 us (2%)
  waiting for transfers between devices  1.33 us (2%)
    pallas_call x1, Pallas kernels, on_device(): pl.pallas_call(functools.partial(term_kernel, width), out_shape=(jax.Shap...  28.3 us
    pallas_call x1, Pallas kernels, on_device(): pl.pallas_call(functools.partial(add_kernel, width, nloc, interior), out_...  19 us
    all_to_all x1, starting transfers between devices, on_device(): gathered = lax.all_to_all(gram, ('px', 'py'), 0, 0)  4.29 us
    ppermute x1, starting transfers between devices, on_device(): back_y = lax.ppermute(side_y, 'py', line_route('py', 1))  3.14 us
    ppermute x1, starting transfers between devices, on_device(): high_y = lax.ppermute(low_y, 'py', line_route('py', -1))  2.08 us
    pallas_call x1, Pallas kernels, on_device(): pl.pallas_call(functools.partial(prepare_kernel, owned_len, face_len, wid...  2.06 us
    unnamed x6, local copies, waits for them, and re-layouts  1.69 us
    ppermute x1, starting transfers between devices, on_device(): back_x = lax.ppermute(side_x, 'px', ring_route('px', 1))  1.52 us
  transfers between devices with their start and end apart: 5, of which 2 were waited for; matrix products, arithmetic and copies ran while one was open for 0% of the time, Pallas kernels for 31%

commit v1 on v0

--- a/solution.py
+++ b/solution.py
@@ -11,6 +11,8 @@
 LANES = 128
 BLOCK_ROWS = 16
 SUB_ROWS = 8
+TERM_MIB = 32
+ADD_MIB = 26
 STEP = 4
 DEEP = 4
 N_ACC = 4
@@ -54,9 +56,9 @@
 
 
 def prepare_kernel(
-    owned_len, face_len, width, count_ref, bloch_ref,
+    owned_len, face_len, width, count_ref, bloch_ref, stiff_elem_ref, mass_elem_ref,
     dofs_ref, pair_ref, stiff_ref, mass_ref,
-    table_ref, own_table_ref, face_table_ref, scale_ref, turn_ref,
+    table_ref, own_table_ref, face_table_ref, scale_ref, turn_ref, coef_ref,
 ):
     nloc, _, capacity = dofs_ref.shape
     face_slots = face_table_ref.shape[1]
@@ -108,6 +110,15 @@
             chooser, jnp.concatenate(split(scales), axis=1)
         )
 
+    curl_lane = iota((8, LANES), 1) // width % 2 == 0
+
+    def build_coef(j, carry):
+        for i in range(nloc):
+            coef_ref[j * nloc + i] = jnp.where(curl_lane, stiff_elem_ref[j, i], mass_elem_ref[j, i])
+        return carry
+
+    lax.fori_loop(0, nloc, build_coef, 0)
+
     ratio = jnp.full((8, LANES), bloch_ref[0].astype(F32), F32) / bloch_ref[1].astype(F32)
     angle = (2.0 * math.pi) * jnp.where(at_end, ratio, 0.0)
     turn_ref[:8] = jnp.cos(angle)
@@ -173,24 +184,27 @@
 
 def term_kernel(
     width,
+    nloc,
     count_ref,
-    stiff_ref,
-    mass_ref,
     table_hbm,
     face_table_hbm,
-    turn_ref,
-    own_ref,
+    turn_hbm,
+    own_hbm,
+    scale_hbm,
+    coef_hbm,
     high_x_ref,
     high_y_ref,
-    scale_ref,
     term_hbm,
     side_x_ref,
     side_y_ref,
     gram_ref,
     dofs_ref,
     face_dofs_ref,
+    turn_ref,
+    own_ref,
+    scale_ref,
+    coef_ref,
     term_ref,
-    coef_ref,
     rows_x,
     gath,
     gram_acc,
@@ -203,19 +217,36 @@
     vecs = width // 2
     groups = LANES // (2 * width)
     capacity = scale_ref.shape[0] * groups
-    nloc = stiff_ref.shape[0]
     face_slots = capacity // 8
     copies = LANES // width
     block_elems = groups * BLOCK_ROWS
     block_terms = nloc * BLOCK_ROWS
 
-    loads = [
-        pltpu.make_async_copy(table_hbm, dofs_ref, sems.at[0]),
-        pltpu.make_async_copy(face_table_hbm, face_dofs_ref, sems.at[1]),
+    own_load, turn_load, *loads = [
+        pltpu.make_async_copy(source, target, sems.at[n])
+        for n, (source, target) in enumerate(
+            (
+                (own_hbm, own_ref),
+                (turn_hbm, turn_ref),
+                (table_hbm, dofs_ref),
+                (face_table_hbm, face_dofs_ref),
+                (coef_hbm, coef_ref),
+                (scale_hbm, scale_ref),
+            )
+        )
     ]
-    for load in loads:
+    for load in (own_load, turn_load, *loads):
         load.start()
 
+    def clear(c, carry):
+        at = pl.ds(pl.multiple_of(c * 4 * LANES, LANES), 4 * LANES)
+        for acc in accs:
+            acc[at, :] = jnp.zeros((4 * LANES, LANES), F32)
+        return carry
+
+    lax.fori_loop(0, face_len // (2 * LANES), clear, 0)
+    gram_acc[...] = jnp.zeros_like(gram_acc)
+    turn_load.wait()
     cos, sin = turn_ref[:vecs], turn_ref[8 : 8 + vecs]
 
     def turned(pair, sign):
@@ -227,8 +258,6 @@
 
     unit = (iota((LANES, LANES), 0) == iota((LANES, LANES), 1)).astype(BF16)
     unit = jnp.concatenate([unit, unit], axis=1)
-    zero_tile = jnp.zeros((LANES, LANES), F32)
-
     def put_rows(tile, first):
         top, low = split(tile)
         tiled = jnp.concatenate(
@@ -245,7 +274,6 @@
             put_rows(own_ref[:, pl.ds(first, LANES)], first)
         return carry
 
-    lax.fori_loop(0, owned_len // (many * LANES), build_own, 0)
 
     def build_face(c, carry):
         for u in range(many // 2):
@@ -258,22 +286,11 @@
                 high_y_ref[:, pl.ds(first, LANES)],
                 pl.multiple_of(owned_len + face_len + first, LANES),
             )
-            for acc in accs:
-                acc[pl.ds(pl.multiple_of(2 * first, 2 * LANES), LANES), :] = zero_tile
-                acc[pl.ds(pl.multiple_of(2 * first + LANES, LANES), LANES), :] = zero_tile
         return carry
 
     lax.fori_loop(0, face_len // (many // 2 * LANES), build_face, 0)
-
-    curl_lane = iota((8, LANES), 1) // width % 2 == 0
-
-    def build_coef(j, carry):
-        for i in range(nloc):
-            coef_ref[j * nloc + i] = jnp.where(curl_lane, stiff_ref[j, i], mass_ref[j, i])
-        return carry
-
-    lax.fori_loop(0, nloc, build_coef, 0)
-    gram_acc[...] = jnp.zeros_like(gram_acc)
+    own_load.wait()
+    lax.fori_loop(0, owned_len // (many * LANES), build_own, 0)
 
     for load in loads:
         load.wait()
@@ -555,7 +572,11 @@
 
     limit = 62 * 1024 * 1024
     params = pltpu.CompilerParams(vmem_limit_bytes=limit)
-    table, own_table, face_table, scale, turn = pl.pallas_call(
+
+    def in_hbm(*values):
+        return [pltpu.with_memory_space_constraint(value, pltpu.HBM) for value in values]
+
+    table, own_table, face_table, scale, turn, coef = pl.pallas_call(
         functools.partial(prepare_kernel, owned_len, face_len, width),
         out_shape=(
             jax.ShapeDtypeStruct((nloc + 1, 1, capacity), jnp.int32),
@@ -563,14 +584,17 @@
             jax.ShapeDtypeStruct((-(-nloc // 8) * 8, face_slots), jnp.int32),
             jax.ShapeDtypeStruct((capacity // groups, LANES), F32),
             jax.ShapeDtypeStruct((16, LANES), F32),
+            jax.ShapeDtypeStruct((nloc * nloc, 8, LANES), F32),
         ),
-        in_specs=[smem] * 2 + [vmem] * 4,
-        out_specs=[vmem] * 5,
+        in_specs=[smem] * 4 + [vmem] * 4,
+        out_specs=[vmem] * 6,
         compiler_params=params,
         name="prepare",
     )(
         live,
         bloch_fraction,
+        stiff_ref,
+        mass_ref,
         elem_dofs.transpose(0, 3, 1, 2).reshape(nloc, 1, capacity),
         pairing.reshape(-1, LANES),
         stiff_coef[0],
@@ -584,32 +608,33 @@
     blocks = capacity // (groups * BLOCK_ROWS)
     term_rows = nloc * capacity // groups
     terms, side_x, side_y, gram = pl.pallas_call(
-        functools.partial(term_kernel, width),
+        functools.partial(term_kernel, width, nloc),
         out_shape=(
-            jax.ShapeDtypeStruct((term_rows, LANES), F32),
+            pltpu.HBM((term_rows, LANES), F32),
             jax.ShapeDtypeStruct((2 * width, face_len), F32),
             jax.ShapeDtypeStruct((2 * width, face_len), F32),
             jax.ShapeDtypeStruct((devices, vecs, LANES), F32),
         ),
-        in_specs=[smem] * 3 + [left] * 2 + [vmem] * 5,
+        in_specs=[smem] + [left] * 6 + [vmem] * 2,
         out_specs=[left] + [vmem] * 3,
         scratch_shapes=[
             pltpu.SMEM(table.shape, jnp.int32),
             pltpu.SMEM(face_table.shape, jnp.int32),
+            pltpu.VMEM(turn.shape, F32),
+            pltpu.VMEM(own_rows.shape, F32),
+            pltpu.VMEM(scale.shape, F32),
+            pltpu.VMEM(coef.shape, F32),
             pltpu.VMEM((term_rows, LANES), F32),
-            pltpu.VMEM((nloc * nloc, 8, LANES), F32),
             pltpu.VMEM((extent, LANES), F32),
             pltpu.VMEM((term_rows, LANES), F32),
             pltpu.VMEM((LANES, LANES), F32),
-            pltpu.SemaphoreType.DMA((2,)),
+            pltpu.SemaphoreType.DMA((6,)),
             pltpu.SemaphoreType.DMA((blocks,)),
         ]
         + [pltpu.VMEM((2 * face_len + 8, LANES), F32)] * N_ACC,
-        compiler_params=pltpu.CompilerParams(vmem_limit_bytes=60 * 1024 * 1024),
+        compiler_params=pltpu.CompilerParams(vmem_limit_bytes=TERM_MIB * 1024 * 1024),
         name="terms",
-    )(
-        live, stiff_ref, mass_ref, table, face_table, turn, own_rows, high_x, high_y, scale
-    )
+    )(live, *in_hbm(table, face_table, turn, own_rows, scale, coef), high_x, high_y)
 
     gathered = lax.all_to_all(gram, ("px", "py"), 0, 0)
     back_x = lax.ppermute(side_x, "px", ring_route("px", 1))
@@ -633,12 +658,12 @@
             pltpu.SemaphoreType.DMA((2 * owned_len // (8 * LANES),)),
         ]
         + [pltpu.VMEM((owned_len + 8, LANES), F32)] * N_ACC,
-        compiler_params=params,
+        compiler_params=pltpu.CompilerParams(vmem_limit_bytes=ADD_MIB * 1024 * 1024),
         cost_estimate=pl.CostEstimate(
             flops=40 * 1024 * 1024 * 1024, bytes_accessed=40 * 1024 * 1024, transcendentals=0
         ),
         name="adds",
-    )(live, own_table, terms)
+    )(live, *in_hbm(own_table, terms))
 
     curl, mass, gram = pl.pallas_call(
         functools.partial(finish_kernel, width, 1.0 / float(devices * owned_len)),

time: 69.2 us -> 66.6 us (0.962)
  the two profiles are of different devices: /device:TPU:17 before, /device:TPU:19 now
where the time goes in v1:
time: 66.6 us; the launch traced here: 66.5 us
  Pallas kernels  52.2 us (78%)
  starting transfers between devices  11.8 us (18%)
  between operations  1.35 us (2%)
  local copies, waits for them, and re-layouts  0.99 us (1%)
    pallas_call x1, Pallas kernels, on_device(): pl.pallas_call(functools.partial(term_kernel, width, nloc), out_shape=(pl...  27.7 us
    pallas_call x1, Pallas kernels, on_device(): pl.pallas_call(functools.partial(add_kernel, width, nloc, interior), out_...  19.5 us
    all_to_all x1, starting transfers between devices, on_device(): gathered = lax.all_to_all(gram, ('px', 'py'), 0, 0)  4 us
    pallas_call x1, Pallas kernels, on_device(): pl.pallas_call(functools.partial(prepare_kernel, owned_len, face_len, wid...  3.49 us
    ppermute x1, starting transfers between devices, on_device(): back_y = lax.ppermute(side_y, 'py', line_route('py', 1))  3.15 us
    ppermute x1, starting transfers between devices, on_device(): high_y = lax.ppermute(low_y, 'py', line_route('py', -1))  2.08 us
    ppermute x1, starting transfers between devices, on_device(): back_x = lax.ppermute(side_x, 'px', ring_route('px', 1))  1.52 us
    pallas_call x1, Pallas kernels, on_device(): pl.pallas_call(functools.partial(finish_kernel, width, 1.0 / float(device...  1.46 us
  transfers between devices with their start and end apart: 5, of which 1 were waited for; matrix products, arithmetic and copies ran while one was open for 0% of the time, Pallas kernels for 35%

profile of v1, /device:TPU:19, one launch (start us, length us, event | category | flops | bytes accessed | tf_op | source)
XLA Modules:
  0.0 66.5 jit_solution(5229636442945522690)
XLA Ops:
  0.6 1.0 %fusion = (f32[16,2048]{1,0:T(8,128)S(1)}, f32[16,2048]{1,0:T(8,128)S(1)}) fusion(f32[16,8192]{1,0:T(8,128)} %bitcast.17), kind=kLoop, calls=%fused_computation | loop fusion | bytes 524288 | tf_op jit(solution)/shard_map/slice | solution.py:565
  1.6 2.1 %collective-permute-start.1 = (f32[16,2048]{1,0:T(8,128)S(1)}, f32[16,2048]{1,0:T(8,128)S(1)}, u32[]{:S(2)}, u32[]{:S(2)}) collective-permute-start(f32[16,2048]{1,0:T(8,128)S(1)} %get-tuple-element.35), channel_id=1, source_target_pairs={{1,0},{2,1},{3,2},{5,4},{6,5},{7,6},{9,8},{10,9},{11,10},{13,12},{... | collective-permute-start | bytes 393224 | tf_op jit(solution)/shard_map/ppermute | solution.py:567
  3.7 1.0 %collective-permute-start = (f32[16,2048]{1,0:T(8,128)S(1)}, f32[16,2048]{1,0:T(8,128)S(1)}, u32[]{:S(2)}, u32[]{:S(2)}) collective-permute-start(f32[16,2048]{1,0:T(8,128)S(1)} %get-tuple-element.36), channel_id=1, source_target_pairs={{0,28},{4,0},{8,4},{12,8},{16,12},{20,16},{24,20},{28,24},{1,29},{... | collective-permute-start | bytes 393224 | tf_op jit(solution)/shard_map/ppermute | solution.py:566
  5.4 3.5 %prepare.1 = (s32[21,1,1024]{2,1,0:T(1,128)}, s32[21,1,1024]{2,1,0:T(1,128)}, s32[24,128]{1,0:T(8,128)}, f32[256,128]{1,0:T(8,128)}, f32[16,128]{1,0:T(8,128)}, /*index=5*/f32[400,8,128]{2,1,0:T(8,128)}) custom-call(s32[1]{0:T(128)} %bitcast.14.count_ref, s32[2]{0:T(128)} %bloch_ref.1, f32[20,20]{1,0:T(8,128)} %stiff_elem_ref.1, f32[20,20]{1,0:T(8,128)} %mass_elem_ref.1, ...), custom_call_target="tpu_custom_call" | custom-call | tf_op jit(solution)/shard_map/prepare/pallas_call | solution.py:579
  8.9 0.0 collective-permute-done.1.high_y_ref
  8.9 0.2 collective-permute-done.high_x_ref
  9.1 27.7 %terms.1 = (f32[5120,128]{1,0:T(8,128)}, f32[32,2048]{1,0:T(8,128)S(1)}, f32[32,2048]{1,0:T(8,128)S(1)}, f32[32,8,128]{2,1,0:T(8,128)}) custom-call(s32[1]{0:T(128)} %bitcast.15.count_ref, s32[21504]{0:T(1024)} %bitcast.21, s32[3072]{0:T(1024)} %bitcast.23, f32[16,128]{1,0:T(8,128)} %get-tuple-element.22.turn_hbm, f32[16,8192]{1,0:T(8,128)} %bitcast.18, ...), custom_call_target="tpu_custom_call" | custom-call | tf_op jit(solution)/shard_map/terms/pallas_call | solution.py:610
  36.7 4.0 %all-to-all-start = ((f32[32,8,128]{2,1,0:T(8,128)}), f32[32,8,128]{2,1,0:T(8,128)S(1)}, u32[]{:S(2)}, u32[]{:S(2)}) async-start(f32[32,8,128]{2,1,0:T(8,128)} %get-tuple-element.31), calls=%async_computation | async-start | bytes 262144 | tf_op jit(solution)/shard_map/all_to_all | solution.py:639
  40.7 1.5 %collective-permute-start.2 = (f32[32,2048]{1,0:T(8,128)S(1)}, f32[32,2048]{1,0:T(8,128)S(1)}, u32[]{:S(2)}, u32[]{:S(2)}) collective-permute-start(f32[32,2048]{1,0:T(8,128)S(1)} %get-tuple-element.29), channel_id=1, source_target_pairs={{0,4},{4,8},{8,12},{12,16},{16,20},{20,24},{24,28},{28,0},{1,5},{5... | collective-permute-start | bytes 786440 | tf_op jit(solution)/shard_map/ppermute | solution.py:640
  42.3 3.1 %collective-permute-start.3 = (f32[32,2048]{1,0:T(8,128)S(1)}, f32[32,2048]{1,0:T(8,128)S(1)}, u32[]{:S(2)}, u32[]{:S(2)}) collective-permute-start(f32[32,2048]{1,0:T(8,128)S(1)} %get-tuple-element.30), channel_id=1, source_target_pairs={{0,1},{1,2},{2,3},{4,5},{5,6},{6,7},{8,9},{9,10},{10,11},{12,13},{... | collective-permute-start | bytes 786440 | tf_op jit(solution)/shard_map/ppermute | solution.py:641
  45.4 19.5 %adds.1 = (f32[16,8192]{1,0:T(8,128)}, f32[16,8192]{1,0:T(8,128)}, f32[2,16,4096]{2,1,0:T(8,128)S(1)}) custom-call(s32[1]{0:T(128)} %bitcast.16.count_ref, s32[21504]{0:T(1024)} %bitcast.27, f32[5120,128]{1,0:T(8,128)} %get-tuple-element.25.term_hbm), custom_call_target="tpu_custom_call" | custom-call | flops 42949672960 | bytes 41943040 | tf_op jit(solution)/shard_map/adds/pallas_call | solution.py:643
  65.0 0.0 all-to-all-done.gram_ref
  65.0 0.0 collective-permute-done.2.back_x_ref
  65.0 0.0 collective-permute-done.3.back_y_ref
  65.0 1.5 %finish.1 = (f32[16,8192]{1,0:T(8,128)}, f32[16,8192]{1,0:T(8,128)}, f32[32,8]{1,0:T(8,128)}) custom-call(f32[16,8192]{1,0:T(8,128)} %get-tuple-element.26.curl_in, f32[16,8192]{1,0:T(8,128)} %get-tuple-element.27.mass_in, f32[2,16,4096]{2,1,0:T(8,128)S(1)} %get-tuple-element.28.face_ref, ...), custom_call_target="tpu_custom_call", output_to_operand_aliasing={{0}: (0, {}), {1}: (1, {})} | custom-call | tf_op jit(solution)/shard_map/finish/pallas_call | solution.py:668
Async XLA Ops:
  1.6 7.2 %collective-permute-start.1 = (f32[16,2048]{1,0:T(8,128)S(1)}, f32[16,2048]{1,0:T(8,128)S(1)}, u32[]{:S(2)}, u32[]{:S(2)}) collective-permute-start(f32[16,2048]{1,0:T(8,128)S(1)} %get-tuple-element.35), channel_id=1, source_target_pairs={{1,0},{2,1},{3,2},{5,4},{6,5},{7,6},{9,8},{10,9},{11,10},{13,12},{... | collective-permute-start | bytes 393224 | tf_op jit(solution)/shard_map/ppermute | solution.py:567
  3.7 5.3 %collective-permute-start = (f32[16,2048]{1,0:T(8,128)S(1)}, f32[16,2048]{1,0:T(8,128)S(1)}, u32[]{:S(2)}, u32[]{:S(2)}) collective-permute-start(f32[16,2048]{1,0:T(8,128)S(1)} %get-tuple-element.36), channel_id=1, source_target_pairs={{0,28},{4,0},{8,4},{12,8},{16,12},{20,16},{24,20},{28,24},{1,29},{... | collective-permute-start | bytes 393224 | tf_op jit(solution)/shard_map/ppermute | solution.py:566
  36.7 28.2 %all-to-all-start = ((f32[32,8,128]{2,1,0:T(8,128)}), f32[32,8,128]{2,1,0:T(8,128)S(1)}, u32[]{:S(2)}, u32[]{:S(2)}) async-start(f32[32,8,128]{2,1,0:T(8,128)} %get-tuple-element.31), calls=%async_computation | async-start | bytes 262144 | tf_op jit(solution)/shard_map/all_to_all | solution.py:639
  40.7 24.2 %collective-permute-start.2 = (f32[32,2048]{1,0:T(8,128)S(1)}, f32[32,2048]{1,0:T(8,128)S(1)}, u32[]{:S(2)}, u32[]{:S(2)}) collective-permute-start(f32[32,2048]{1,0:T(8,128)S(1)} %get-tuple-element.29), channel_id=1, source_target_pairs={{0,4},{4,8},{8,12},{12,16},{16,20},{20,24},{24,28},{28,0},{1,5},{5... | collective-permute-start | bytes 786440 | tf_op jit(solution)/shard_map/ppermute | solution.py:640
  42.3 22.7 %collective-permute-start.3 = (f32[32,2048]{1,0:T(8,128)S(1)}, f32[32,2048]{1,0:T(8,128)S(1)}, u32[]{:S(2)}, u32[]{:S(2)}) collective-permute-start(f32[32,2048]{1,0:T(8,128)S(1)} %get-tuple-element.30), channel_id=1, source_target_pairs={{0,1},{1,2},{2,3},{4,5},{5,6},{6,7},{8,9},{9,10},{10,11},{12,13},{... | collective-permute-start | bytes 786440 | tf_op jit(solution)/shard_map/ppermute | solution.py:641

commit v2 on v1

--- a/solution.py
+++ b/solution.py
@@ -8,9 +8,11 @@
 from jax.experimental.pallas import tpu as pltpu
 from jax.sharding import PartitionSpec as P
 
+
 LANES = 128
 BLOCK_ROWS = 16
 SUB_ROWS = 8
+PAIR = 2
 TERM_MIB = 32
 ADD_MIB = 26
 STEP = 4
@@ -58,7 +60,7 @@
 def prepare_kernel(
     owned_len, face_len, width, count_ref, bloch_ref, stiff_elem_ref, mass_elem_ref,
     dofs_ref, pair_ref, stiff_ref, mass_ref,
-    table_ref, own_table_ref, face_table_ref, scale_ref, turn_ref, coef_ref,
+    table_ref, own_table_ref, face_table_ref, scale_ref, turn_ref, coef_hbm, coef_ref, coef_sem,
 ):
     nloc, _, capacity = dofs_ref.shape
     face_slots = face_table_ref.shape[1]
@@ -66,17 +68,29 @@
     at_end = lax.axis_index("px") == lax.axis_size("px") - 1
     live = count_ref[0]
 
+    curl_lane = iota((8, LANES), 1) // width % 2 == 0
+
+    def build_coef(j, carry):
+        for i in range(nloc):
+            coef_ref[j * nloc + i] = jnp.where(curl_lane, stiff_elem_ref[j, i], mass_elem_ref[j, i])
+        return carry
+
+    lax.fori_loop(0, nloc, build_coef, 0)
+    coef_move = pltpu.make_async_copy(coef_ref, coef_hbm, coef_sem)
+    coef_move.start()
+
     index = [dofs_ref[i] for i in range(nloc)]
     flag = jnp.zeros((1, capacity), jnp.int32)
     for i in range(nloc):
         for k in range(i + 1, min(i // STEP * STEP + STEP, nloc)):
             flag = jnp.where(index[i] == index[k], 1, flag)
-    reach = groups * SUB_ROWS // 2
-    while reach:
-        flag = jnp.maximum(flag, pltpu.roll(flag, reach, 1))
-        reach //= 2
-    table_ref[nloc] = flag
-    own_table_ref[nloc] = flag
+    reach = 1
+    for row, rows in ((1, PAIR), (0, SUB_ROWS)):
+        while reach < groups * rows:
+            flag = jnp.maximum(flag, pltpu.roll(flag, reach, 1))
+            reach *= 2
+        table_ref[nloc + row] = flag
+        own_table_ref[nloc + row] = flag
     for i in range(nloc):
         table_ref[i] = index[i]
         own_table_ref[i] = jnp.minimum(index[i], owned_len)
@@ -110,19 +124,11 @@
             chooser, jnp.concatenate(split(scales), axis=1)
         )
 
-    curl_lane = iota((8, LANES), 1) // width % 2 == 0
-
-    def build_coef(j, carry):
-        for i in range(nloc):
-            coef_ref[j * nloc + i] = jnp.where(curl_lane, stiff_elem_ref[j, i], mass_elem_ref[j, i])
-        return carry
-
-    lax.fori_loop(0, nloc, build_coef, 0)
-
     ratio = jnp.full((8, LANES), bloch_ref[0].astype(F32), F32) / bloch_ref[1].astype(F32)
     angle = (2.0 * math.pi) * jnp.where(at_end, ratio, 0.0)
     turn_ref[:8] = jnp.cos(angle)
     turn_ref[8:] = jnp.sin(angle)
+    coef_move.wait()
 
 
 def lane_masks(width, groups):
@@ -143,42 +149,53 @@
     return jnp.concatenate([folder, folder], axis=1)
 
 
-def add_block(term_ref, accs, index_of, b, nloc, groups):
-    unroll = 2
-
-    def run(step, first_row, first_elem):
-        def some(t, c):
-            for u in range(unroll):
-                g = t * unroll + u
+def add_block(term_ref, accs, index_of, flag_of, b, nloc, groups):
+    def part(h, carry):
+        first_row = b * nloc * BLOCK_ROWS + h * SUB_ROWS
+        first_elem = (b * (BLOCK_ROWS // SUB_ROWS) + h) * SUB_ROWS * groups
+
+        def add_pair(t, step):
+            for u in range(PAIR):
+                g = t * PAIR + u
                 elem = first_elem + g * groups
                 for j in range(0, nloc, step):
                     slots = range(j, min(j + step, nloc))
                     new = [term_ref[pl.ds(first_row + s * BLOCK_ROWS + g, 1), :] for s in slots]
                     for k in range(groups):
-                        places = [pl.ds(index_of[0](s, elem + k), 1) for s in slots]
+                        places = [pl.ds(index_of(s, elem + k), 1) for s in slots]
                         sums = [accs[k][at, :] + row for at, row in zip(places, new)]
                         for at, row in zip(places, sums):
                             accs[k][at, :] = row
+
+        def plain(t, c):
+            add_pair(t, STEP)
             return c
 
-        lax.fori_loop(0, SUB_ROWS // unroll, some, 0)
-
-    def part(h, carry):
-        first_row = b * nloc * BLOCK_ROWS + h * SUB_ROWS
-        first_elem = (b * (BLOCK_ROWS // SUB_ROWS) + h) * SUB_ROWS * groups
-        clash = index_of[1](nloc, first_elem + SUB_ROWS * groups - 1)
+        def careful(t, c):
+            repeated = flag_of(nloc + 1, first_elem + (t + 1) * PAIR * groups - 1)
+
+            @pl.when(repeated == 0)
+            def _():
+                add_pair(t, STEP)
+
+            @pl.when(repeated != 0)
+            def _():
+                add_pair(t, 1)
+
+            return c
+
+        clash = flag_of(nloc, first_elem + SUB_ROWS * groups - 1)
 
         @pl.when(clash == 0)
         def _():
-            run(STEP, first_row, first_elem)
+            lax.fori_loop(0, SUB_ROWS // PAIR, plain, 0)
 
         @pl.when(clash != 0)
         def _():
-            run(1, first_row, first_elem)
-
-        return carry
-
-    index_of = index_of if isinstance(index_of, tuple) else (index_of, index_of)
+            lax.fori_loop(0, SUB_ROWS // PAIR, careful, 0)
+
+        return carry
+
     lax.fori_loop(0, BLOCK_ROWS // SUB_ROWS, part, 0)
 
 
@@ -258,6 +275,7 @@
 
     unit = (iota((LANES, LANES), 0) == iota((LANES, LANES), 1)).astype(BF16)
     unit = jnp.concatenate([unit, unit], axis=1)
+
     def put_rows(tile, first):
         top, low = split(tile)
         tiled = jnp.concatenate(
@@ -348,12 +366,13 @@
         return pltpu.make_async_copy(term_ref.at[at], term_hbm.at[at], term_sems.at[b])
 
     def face_block(b, carry):
-        add_block(term_ref, accs, (face_index_of, index_of), b, nloc, groups)
+        add_block(term_ref, accs, face_index_of, index_of, b, nloc, groups)
         return carry
 
     live = count_ref[0]
     blocks = (live + block_elems - 1) // block_elems
     face_blocks = jnp.minimum(blocks, face_slots // block_elems)
+
     def full_block(b, carry):
         block(b, True)
 
@@ -402,8 +421,8 @@
         return dot_nt(folder, jnp.concatenate(split(total), axis=1))
 
     def fold_face(c, carry):
-        for u in range(2):
-            first = pl.multiple_of((2 * c + u) * wide, wide)
+        for u in range(4):
+            first = pl.multiple_of((4 * c + u) * wide, wide)
             at = pl.ds(first, wide)
             total = folded(first)
             side_x_ref[:width, at] = turned(total[:width], -1.0)
@@ -411,7 +430,7 @@
             side_y_ref[:, at] = folded(pl.multiple_of(face_len + first, wide))
         return carry
 
-    lax.fori_loop(0, face_len // (2 * wide), fold_face, 0)
+    lax.fori_loop(0, face_len // (4 * wide), fold_face, 0)
 
     whole = gram_acc[...]
     total = whole[:width]
@@ -475,7 +494,7 @@
 
     def block(b, carry):
         fetch(b).wait()
-        add_block(term_ref, accs, index_of, b, nloc, groups)
+        add_block(term_ref, accs, index_of, index_of, b, nloc, groups)
         return carry
 
     lax.fori_loop(0, blocks, block, 0)
@@ -579,15 +598,19 @@
     table, own_table, face_table, scale, turn, coef = pl.pallas_call(
         functools.partial(prepare_kernel, owned_len, face_len, width),
         out_shape=(
-            jax.ShapeDtypeStruct((nloc + 1, 1, capacity), jnp.int32),
-            jax.ShapeDtypeStruct((nloc + 1, 1, capacity), jnp.int32),
+            jax.ShapeDtypeStruct((nloc + 2, 1, capacity), jnp.int32),
+            jax.ShapeDtypeStruct((nloc + 2, 1, capacity), jnp.int32),
             jax.ShapeDtypeStruct((-(-nloc // 8) * 8, face_slots), jnp.int32),
             jax.ShapeDtypeStruct((capacity // groups, LANES), F32),
             jax.ShapeDtypeStruct((16, LANES), F32),
             jax.ShapeDtypeStruct((nloc * nloc, 8, LANES), F32),
         ),
         in_specs=[smem] * 4 + [vmem] * 4,
-        out_specs=[vmem] * 6,
+        out_specs=[vmem] * 5 + [left],
+        scratch_shapes=[
+            pltpu.VMEM((nloc * nloc, 8, LANES), F32),
+            pltpu.SemaphoreType.DMA,
+        ],
         compiler_params=params,
         name="prepare",
     )(
@@ -636,9 +659,9 @@
         name="terms",
     )(live, *in_hbm(table, face_table, turn, own_rows, scale, coef), high_x, high_y)
 
-    gathered = lax.all_to_all(gram, ("px", "py"), 0, 0)
     back_x = lax.ppermute(side_x, "px", ring_route("px", 1))
     back_y = lax.ppermute(side_y, "py", line_route("py", 1))
+    gathered = lax.all_to_all(gram, ("px", "py"), 0, 0)
 
     curl, mass, faces = pl.pallas_call(
         functools.partial(add_kernel, width, nloc, interior),

time: 66.6 us -> 64.8 us (0.973)
  Pallas kernels: 52.2 us -> 49.5 us
  starting transfers between devices: 11.8 us -> 12.5 us
    pallas_call x1, Pallas kernels: 19.5 us -> 17.5 us  [on_device(): pl.pallas_call(functools.partial(add_kernel, width, nloc, interior), out_...]
    pallas_call x1, Pallas kernels: 27.7 us -> 26.9 us  [on_device(): pl.pallas_call(functools.partial(term_kernel, width, nloc), out_shape=(pl...]
    all_to_all x1, starting transfers between devices: 4 us -> 4.79 us  [on_device(): gathered = lax.all_to_all(gram, ('px', 'py'), 0, 0)]
  transfers between devices with their start and end apart: 5 -> 5, of which waited for: 1 -> 0; matrix products, arithmetic and copies ran while one was open for 0% -> 0% of each run, Pallas kernels for 35% -> 33%
where the time goes in v2:
time: 64.8 us; the launch traced here: 64.4 us
  Pallas kernels  49.5 us (76%)
  starting transfers between devices  12.5 us (19%)
  between operations  1.36 us (2%)
  local copies, waits for them, and re-layouts  0.99 us (2%)
    pallas_call x1, Pallas kernels, on_device(): pl.pallas_call(functools.partial(term_kernel, width, nloc), out_shape=(pl...  26.9 us
    pallas_call x1, Pallas kernels, on_device(): pl.pallas_call(functools.partial(add_kernel, width, nloc, interior), out_...  17.5 us
    all_to_all x1, starting transfers between devices, on_device(): gathered = lax.all_to_all(gram, ('px', 'py'), 0, 0)  4.79 us
    pallas_call x1, Pallas kernels, on_device(): pl.pallas_call(functools.partial(prepare_kernel, owned_len, face_len, wid...  3.65 us
    ppermute x1, starting transfers between devices, on_device(): back_y = lax.ppermute(side_y, 'py', line_route('py', 1))  3.15 us
    ppermute x1, starting transfers between devices, on_device(): high_y = lax.ppermute(low_y, 'py', line_route('py', -1))  2.08 us
    ppermute x1, starting transfers between devices, on_device(): back_x = lax.ppermute(side_x, 'px', ring_route('px', 1))  1.52 us
    pallas_call x1, Pallas kernels, on_device(): pl.pallas_call(functools.partial(finish_kernel, width, 1.0 / float(device...  1.46 us
  transfers between devices with their start and end apart: 5, of which 0 were waited for; matrix products, arithmetic and copies ran while one was open for 0% of the time, Pallas kernels for 33%

profile of v2, /device:TPU:19, one launch (start us, length us, event | category | flops | bytes accessed | tf_op | source)
XLA Modules:
  0.0 64.4 jit_solution(1916044378846733373)
XLA Ops:
  0.6 1.0 %fusion = (f32[16,2048]{1,0:T(8,128)S(1)}, f32[16,2048]{1,0:T(8,128)S(1)}) fusion(f32[16,8192]{1,0:T(8,128)} %bitcast.17), kind=kLoop, calls=%fused_computation | loop fusion | bytes 524288 | tf_op jit(solution)/shard_map/slice | solution.py:584
  1.6 2.1 %collective-permute-start.1 = (f32[16,2048]{1,0:T(8,128)S(1)}, f32[16,2048]{1,0:T(8,128)S(1)}, u32[]{:S(2)}, u32[]{:S(2)}) collective-permute-start(f32[16,2048]{1,0:T(8,128)S(1)} %get-tuple-element.35), channel_id=1, source_target_pairs={{1,0},{2,1},{3,2},{5,4},{6,5},{7,6},{9,8},{10,9},{11,10},{13,12},{... | collective-permute-start | bytes 393224 | tf_op jit(solution)/shard_map/ppermute | solution.py:586
  3.7 1.0 %collective-permute-start = (f32[16,2048]{1,0:T(8,128)S(1)}, f32[16,2048]{1,0:T(8,128)S(1)}, u32[]{:S(2)}, u32[]{:S(2)}) collective-permute-start(f32[16,2048]{1,0:T(8,128)S(1)} %get-tuple-element.36), channel_id=1, source_target_pairs={{0,28},{4,0},{8,4},{12,8},{16,12},{20,16},{24,20},{28,24},{1,29},{... | collective-permute-start | bytes 393224 | tf_op jit(solution)/shard_map/ppermute | solution.py:585
  5.4 3.6 %prepare.1 = (s32[22,1,1024]{2,1,0:T(1,128)}, s32[22,1,1024]{2,1,0:T(1,128)}, s32[24,128]{1,0:T(8,128)}, f32[256,128]{1,0:T(8,128)}, f32[16,128]{1,0:T(8,128)}, /*index=5*/f32[400,8,128]{2,1,0:T(8,128)}) custom-call(s32[1]{0:T(128)} %bitcast.14.count_ref, s32[2]{0:T(128)} %bloch_ref.1, f32[20,20]{1,0:T(8,128)} %stiff_elem_ref.1, f32[20,20]{1,0:T(8,128)} %mass_elem_ref.1, ...), custom_call_target="tpu_custom_call" | custom-call | tf_op jit(solution)/shard_map/prepare/pallas_call | solution.py:598
  9.0 0.0 collective-permute-done.1.high_y_ref
  9.0 0.0 collective-permute-done.high_x_ref
  9.1 26.9 %terms.1 = (f32[5120,128]{1,0:T(8,128)}, f32[32,2048]{1,0:T(8,128)S(1)}, f32[32,2048]{1,0:T(8,128)S(1)}, f32[32,8,128]{2,1,0:T(8,128)}) custom-call(s32[1]{0:T(128)} %bitcast.15.count_ref, s32[22528]{0:T(1024)} %bitcast.21, s32[3072]{0:T(1024)} %bitcast.23, f32[16,128]{1,0:T(8,128)} %get-tuple-element.22.turn_hbm, f32[16,8192]{1,0:T(8,128)} %bitcast.18, ...), custom_call_target="tpu_custom_call" | custom-call | tf_op jit(solution)/shard_map/terms/pallas_call | solution.py:633
  35.9 4.8 %all-to-all-start = ((f32[32,8,128]{2,1,0:T(8,128)}), f32[32,8,128]{2,1,0:T(8,128)S(1)}, u32[]{:S(2)}, u32[]{:S(2)}) async-start(f32[32,8,128]{2,1,0:T(8,128)} %get-tuple-element.31), calls=%async_computation | async-start | bytes 262144 | tf_op jit(solution)/shard_map/all_to_all | solution.py:664
  40.7 1.5 %collective-permute-start.2 = (f32[32,2048]{1,0:T(8,128)S(1)}, f32[32,2048]{1,0:T(8,128)S(1)}, u32[]{:S(2)}, u32[]{:S(2)}) collective-permute-start(f32[32,2048]{1,0:T(8,128)S(1)} %get-tuple-element.29), channel_id=1, source_target_pairs={{0,4},{4,8},{8,12},{12,16},{16,20},{20,24},{24,28},{28,0},{1,5},{5... | collective-permute-start | bytes 786440 | tf_op jit(solution)/shard_map/ppermute | solution.py:662
  42.3 3.1 %collective-permute-start.3 = (f32[32,2048]{1,0:T(8,128)S(1)}, f32[32,2048]{1,0:T(8,128)S(1)}, u32[]{:S(2)}, u32[]{:S(2)}) collective-permute-start(f32[32,2048]{1,0:T(8,128)S(1)} %get-tuple-element.30), channel_id=1, source_target_pairs={{0,1},{1,2},{2,3},{4,5},{5,6},{6,7},{8,9},{9,10},{10,11},{12,13},{... | collective-permute-start | bytes 786440 | tf_op jit(solution)/shard_map/ppermute | solution.py:663
  45.4 17.5 %adds.1 = (f32[16,8192]{1,0:T(8,128)}, f32[16,8192]{1,0:T(8,128)}, f32[2,16,4096]{2,1,0:T(8,128)S(1)}) custom-call(s32[1]{0:T(128)} %bitcast.16.count_ref, s32[22528]{0:T(1024)} %bitcast.27, f32[5120,128]{1,0:T(8,128)} %get-tuple-element.25.term_hbm), custom_call_target="tpu_custom_call" | custom-call | flops 42949672960 | bytes 41943040 | tf_op jit(solution)/shard_map/adds/pallas_call | solution.py:666
  62.9 0.0 all-to-all-done.gram_ref
  62.9 0.0 collective-permute-done.2.back_x_ref
  62.9 0.0 collective-permute-done.3.back_y_ref
  62.9 1.5 %finish.1 = (f32[16,8192]{1,0:T(8,128)}, f32[16,8192]{1,0:T(8,128)}, f32[32,8]{1,0:T(8,128)}) custom-call(f32[16,8192]{1,0:T(8,128)} %get-tuple-element.26.curl_in, f32[16,8192]{1,0:T(8,128)} %get-tuple-element.27.mass_in, f32[2,16,4096]{2,1,0:T(8,128)S(1)} %get-tuple-element.28.face_ref, ...), custom_call_target="tpu_custom_call", output_to_operand_aliasing={{0}: (0, {}), {1}: (1, {})} | custom-call | tf_op jit(solution)/shard_map/finish/pallas_call | solution.py:691
Async XLA Ops:
  1.6 7.4 %collective-permute-start.1 = (f32[16,2048]{1,0:T(8,128)S(1)}, f32[16,2048]{1,0:T(8,128)S(1)}, u32[]{:S(2)}, u32[]{:S(2)}) collective-permute-start(f32[16,2048]{1,0:T(8,128)S(1)} %get-tuple-element.35), channel_id=1, source_target_pairs={{1,0},{2,1},{3,2},{5,4},{6,5},{7,6},{9,8},{10,9},{11,10},{13,12},{... | collective-permute-start | bytes 393224 | tf_op jit(solution)/shard_map/ppermute | solution.py:586
  3.7 5.3 %collective-permute-start = (f32[16,2048]{1,0:T(8,128)S(1)}, f32[16,2048]{1,0:T(8,128)S(1)}, u32[]{:S(2)}, u32[]{:S(2)}) collective-permute-start(f32[16,2048]{1,0:T(8,128)S(1)} %get-tuple-element.36), channel_id=1, source_target_pairs={{0,28},{4,0},{8,4},{12,8},{16,12},{20,16},{24,20},{28,24},{1,29},{... | collective-permute-start | bytes 393224 | tf_op jit(solution)/shard_map/ppermute | solution.py:585
  35.9 27.0 %all-to-all-start = ((f32[32,8,128]{2,1,0:T(8,128)}), f32[32,8,128]{2,1,0:T(8,128)S(1)}, u32[]{:S(2)}, u32[]{:S(2)}) async-start(f32[32,8,128]{2,1,0:T(8,128)} %get-tuple-element.31), calls=%async_computation | async-start | bytes 262144 | tf_op jit(solution)/shard_map/all_to_all | solution.py:664
  40.7 22.2 %collective-permute-start.2 = (f32[32,2048]{1,0:T(8,128)S(1)}, f32[32,2048]{1,0:T(8,128)S(1)}, u32[]{:S(2)}, u32[]{:S(2)}) collective-permute-start(f32[32,2048]{1,0:T(8,128)S(1)} %get-tuple-element.29), channel_id=1, source_target_pairs={{0,4},{4,8},{8,12},{12,16},{16,20},{20,24},{24,28},{28,0},{1,5},{5... | collective-permute-start | bytes 786440 | tf_op jit(solution)/shard_map/ppermute | solution.py:662
  42.3 20.7 %collective-permute-start.3 = (f32[32,2048]{1,0:T(8,128)S(1)}, f32[32,2048]{1,0:T(8,128)S(1)}, u32[]{:S(2)}, u32[]{:S(2)}) collective-permute-start(f32[32,2048]{1,0:T(8,128)S(1)} %get-tuple-element.30), channel_id=1, source_target_pairs={{0,1},{1,2},{2,3},{4,5},{5,6},{6,7},{8,9},{9,10},{10,11},{12,13},{... | collective-permute-start | bytes 786440 | tf_op jit(solution)/shard_map/ppermute | solution.py:663

commit v3 on v2

--- a/solution.py
+++ b/solution.py
@@ -541,10 +541,13 @@
     face_len = back_x_ref.shape[1]
     outer = pl.ds(curl_out.shape[1] - 2 * face_len, 2 * face_len)
     moves = []
+    at_start = lax.axis_index("py") == 0
     for n, image in enumerate((curl_out, mass_out)):
         rows = slice(n * width, (n + 1) * width)
         faces[n, :, :face_len] = face_ref[n, :, :face_len] + back_x_ref[rows, :]
-        faces[n, :, face_len:] = face_ref[n, :, face_len:] + back_y_ref[rows, :]
+        faces[n, :, face_len:] = face_ref[n, :, face_len:] + jnp.where(
+            at_start, 0.0, back_y_ref[rows, :]
+        )
         moves.append(pltpu.make_async_copy(faces.at[n], image.at[:, outer], sems.at[n]))
         moves[-1].start()
     total = gram_ref[0]
@@ -660,7 +663,7 @@
     )(live, *in_hbm(table, face_table, turn, own_rows, scale, coef), high_x, high_y)
 
     back_x = lax.ppermute(side_x, "px", ring_route("px", 1))
-    back_y = lax.ppermute(side_y, "py", line_route("py", 1))
+    back_y = lax.ppermute(side_y, "py", ring_route("py", 1))
     gathered = lax.all_to_all(gram, ("px", "py"), 0, 0)
 
     curl, mass, faces = pl.pallas_call(

time: 64.8 us -> 62.8 us (0.969)
  starting transfers between devices: 12.5 us -> 10.7 us
    ppermute x1, starting transfers between devices: 3.15 us -> 1.25 us  [on_device(): back_y = lax.ppermute(side_y, 'py', ring_route('py', 1))]
  transfers between devices with their start and end apart: 5 -> 5, of which waited for: 0 -> 0; matrix products, arithmetic and copies ran while one was open for 0% -> 0% of each run, Pallas kernels for 33% -> 34%
where the time goes in v3:
time: 62.8 us; the launch traced here: 62.5 us
  Pallas kernels  49.5 us (79%)
  starting transfers between devices  10.7 us (17%)
  between operations  1.36 us (2%)
  local copies, waits for them, and re-layouts  0.99 us (2%)
    pallas_call x1, Pallas kernels, on_device(): pl.pallas_call(functools.partial(term_kernel, width, nloc), out_shape=(pl...  26.9 us
    pallas_call x1, Pallas kernels, on_device(): pl.pallas_call(functools.partial(add_kernel, width, nloc, interior), out_...  17.5 us
    all_to_all x1, starting transfers between devices, on_device(): gathered = lax.all_to_all(gram, ('px', 'py'), 0, 0)  4.79 us
    pallas_call x1, Pallas kernels, on_device(): pl.pallas_call(functools.partial(prepare_kernel, owned_len, face_len, wid...  3.65 us
    ppermute x1, starting transfers between devices, on_device(): high_y = lax.ppermute(low_y, 'py', line_route('py', -1))  2.08 us
    ppermute x1, starting transfers between devices, on_device(): back_x = lax.ppermute(side_x, 'px', ring_route('px', 1))  1.52 us
    pallas_call x1, Pallas kernels, on_device(): pl.pallas_call(functools.partial(finish_kernel, width, 1.0 / float(device...  1.46 us
  transfers between devices with their start and end apart: 5, of which 0 were waited for; matrix products, arithmetic and copies ran while one was open for 0% of the time, Pallas kernels for 34%

profile of v3, /device:TPU:19, one launch (start us, length us, event | category | flops | bytes accessed | tf_op | source)
XLA Modules:
  0.0 62.5 jit_solution(11338390186121007565)
XLA Ops:
  0.6 1.0 %fusion = (f32[16,2048]{1,0:T(8,128)S(1)}, f32[16,2048]{1,0:T(8,128)S(1)}) fusion(f32[16,8192]{1,0:T(8,128)} %bitcast.17), kind=kLoop, calls=%fused_computation | loop fusion | bytes 524288 | tf_op jit(solution)/shard_map/slice | solution.py:587
  1.6 2.1 %collective-permute-start.1 = (f32[16,2048]{1,0:T(8,128)S(1)}, f32[16,2048]{1,0:T(8,128)S(1)}, u32[]{:S(2)}, u32[]{:S(2)}) collective-permute-start(f32[16,2048]{1,0:T(8,128)S(1)} %get-tuple-element.35), channel_id=1, source_target_pairs={{1,0},{2,1},{3,2},{5,4},{6,5},{7,6},{9,8},{10,9},{11,10},{13,12},{... | collective-permute-start | bytes 393224 | tf_op jit(solution)/shard_map/ppermute | solution.py:589
  3.7 1.0 %collective-permute-start = (f32[16,2048]{1,0:T(8,128)S(1)}, f32[16,2048]{1,0:T(8,128)S(1)}, u32[]{:S(2)}, u32[]{:S(2)}) collective-permute-start(f32[16,2048]{1,0:T(8,128)S(1)} %get-tuple-element.36), channel_id=1, source_target_pairs={{0,28},{4,0},{8,4},{12,8},{16,12},{20,16},{24,20},{28,24},{1,29},{... | collective-permute-start | bytes 393224 | tf_op jit(solution)/shard_map/ppermute | solution.py:588
  5.4 3.6 %prepare.1 = (s32[22,1,1024]{2,1,0:T(1,128)}, s32[22,1,1024]{2,1,0:T(1,128)}, s32[24,128]{1,0:T(8,128)}, f32[256,128]{1,0:T(8,128)}, f32[16,128]{1,0:T(8,128)}, /*index=5*/f32[400,8,128]{2,1,0:T(8,128)}) custom-call(s32[1]{0:T(128)} %bitcast.14.count_ref, s32[2]{0:T(128)} %bloch_ref.1, f32[20,20]{1,0:T(8,128)} %stiff_elem_ref.1, f32[20,20]{1,0:T(8,128)} %mass_elem_ref.1, ...), custom_call_target="tpu_custom_call" | custom-call | tf_op jit(solution)/shard_map/prepare/pallas_call | solution.py:601
  9.0 0.0 collective-permute-done.1.high_y_ref
  9.0 0.0 collective-permute-done.high_x_ref
  9.1 26.9 %terms.1 = (f32[5120,128]{1,0:T(8,128)}, f32[32,2048]{1,0:T(8,128)S(1)}, f32[32,2048]{1,0:T(8,128)S(1)}, f32[32,8,128]{2,1,0:T(8,128)}) custom-call(s32[1]{0:T(128)} %bitcast.15.count_ref, s32[22528]{0:T(1024)} %bitcast.21, s32[3072]{0:T(1024)} %bitcast.23, f32[16,128]{1,0:T(8,128)} %get-tuple-element.22.turn_hbm, f32[16,8192]{1,0:T(8,128)} %bitcast.18, ...), custom_call_target="tpu_custom_call" | custom-call | tf_op jit(solution)/shard_map/terms/pallas_call | solution.py:636
  35.9 4.8 %all-to-all-start = ((f32[32,8,128]{2,1,0:T(8,128)}), f32[32,8,128]{2,1,0:T(8,128)S(1)}, u32[]{:S(2)}, u32[]{:S(2)}) async-start(f32[32,8,128]{2,1,0:T(8,128)} %get-tuple-element.31), calls=%async_computation | async-start | bytes 262144 | tf_op jit(solution)/shard_map/all_to_all | solution.py:667
  40.7 1.5 %collective-permute-start.2 = (f32[32,2048]{1,0:T(8,128)S(1)}, f32[32,2048]{1,0:T(8,128)S(1)}, u32[]{:S(2)}, u32[]{:S(2)}) collective-permute-start(f32[32,2048]{1,0:T(8,128)S(1)} %get-tuple-element.29), channel_id=1, source_target_pairs={{0,4},{4,8},{8,12},{12,16},{16,20},{20,24},{24,28},{28,0},{1,5},{5... | collective-permute-start | bytes 786440 | tf_op jit(solution)/shard_map/ppermute | solution.py:665
  42.3 1.2 %collective-permute-start.3 = (f32[32,2048]{1,0:T(8,128)S(1)}, f32[32,2048]{1,0:T(8,128)S(1)}, u32[]{:S(2)}, u32[]{:S(2)}) collective-permute-start(f32[32,2048]{1,0:T(8,128)S(1)} %get-tuple-element.30), channel_id=1, source_target_pairs={{0,1},{1,2},{2,3},{3,0},{4,5},{5,6},{6,7},{7,4},{8,9},{9,10},{10,1... | collective-permute-start | bytes 786440 | tf_op jit(solution)/shard_map/ppermute | solution.py:666
  43.5 17.5 %adds.1 = (f32[16,8192]{1,0:T(8,128)}, f32[16,8192]{1,0:T(8,128)}, f32[2,16,4096]{2,1,0:T(8,128)S(1)}) custom-call(s32[1]{0:T(128)} %bitcast.16.count_ref, s32[22528]{0:T(1024)} %bitcast.27, f32[5120,128]{1,0:T(8,128)} %get-tuple-element.25.term_hbm), custom_call_target="tpu_custom_call" | custom-call | flops 42949672960 | bytes 41943040 | tf_op jit(solution)/shard_map/adds/pallas_call | solution.py:669
  61.0 0.0 all-to-all-done.gram_ref
  61.0 0.0 collective-permute-done.2.back_x_ref
  61.0 0.0 collective-permute-done.3.back_y_ref
  61.0 1.5 %finish.1 = (f32[16,8192]{1,0:T(8,128)}, f32[16,8192]{1,0:T(8,128)}, f32[32,8]{1,0:T(8,128)}) custom-call(f32[16,8192]{1,0:T(8,128)} %get-tuple-element.26.curl_in, f32[16,8192]{1,0:T(8,128)} %get-tuple-element.27.mass_in, f32[2,16,4096]{2,1,0:T(8,128)S(1)} %get-tuple-element.28.face_ref, ...), custom_call_target="tpu_custom_call", output_to_operand_aliasing={{0}: (0, {}), {1}: (1, {})} | custom-call | tf_op jit(solution)/shard_map/finish/pallas_call | solution.py:694
Async XLA Ops:
  1.6 7.4 %collective-permute-start.1 = (f32[16,2048]{1,0:T(8,128)S(1)}, f32[16,2048]{1,0:T(8,128)S(1)}, u32[]{:S(2)}, u32[]{:S(2)}) collective-permute-start(f32[16,2048]{1,0:T(8,128)S(1)} %get-tuple-element.35), channel_id=1, source_target_pairs={{1,0},{2,1},{3,2},{5,4},{6,5},{7,6},{9,8},{10,9},{11,10},{13,12},{... | collective-permute-start | bytes 393224 | tf_op jit(solution)/shard_map/ppermute | solution.py:589
  3.7 5.3 %collective-permute-start = (f32[16,2048]{1,0:T(8,128)S(1)}, f32[16,2048]{1,0:T(8,128)S(1)}, u32[]{:S(2)}, u32[]{:S(2)}) collective-permute-start(f32[16,2048]{1,0:T(8,128)S(1)} %get-tuple-element.36), channel_id=1, source_target_pairs={{0,28},{4,0},{8,4},{12,8},{16,12},{20,16},{24,20},{28,24},{1,29},{... | collective-permute-start | bytes 393224 | tf_op jit(solution)/shard_map/ppermute | solution.py:588
  35.9 25.1 %all-to-all-start = ((f32[32,8,128]{2,1,0:T(8,128)}), f32[32,8,128]{2,1,0:T(8,128)S(1)}, u32[]{:S(2)}, u32[]{:S(2)}) async-start(f32[32,8,128]{2,1,0:T(8,128)} %get-tuple-element.31), calls=%async_computation | async-start | bytes 262144 | tf_op jit(solution)/shard_map/all_to_all | solution.py:667
  40.7 20.3 %collective-permute-start.2 = (f32[32,2048]{1,0:T(8,128)S(1)}, f32[32,2048]{1,0:T(8,128)S(1)}, u32[]{:S(2)}, u32[]{:S(2)}) collective-permute-start(f32[32,2048]{1,0:T(8,128)S(1)} %get-tuple-element.29), channel_id=1, source_target_pairs={{0,4},{4,8},{8,12},{12,16},{16,20},{20,24},{24,28},{28,0},{1,5},{5... | collective-permute-start | bytes 786440 | tf_op jit(solution)/shard_map/ppermute | solution.py:665
  42.3 18.8 %collective-permute-start.3 = (f32[32,2048]{1,0:T(8,128)S(1)}, f32[32,2048]{1,0:T(8,128)S(1)}, u32[]{:S(2)}, u32[]{:S(2)}) collective-permute-start(f32[32,2048]{1,0:T(8,128)S(1)} %get-tuple-element.30), channel_id=1, source_target_pairs={{0,1},{1,2},{2,3},{3,0},{4,5},{5,6},{6,7},{7,4},{8,9},{9,10},{10,1... | collective-permute-start | bytes 786440 | tf_op jit(solution)/shard_map/ppermute | solution.py:666

commit v4 on v3

--- a/solution.py
+++ b/solution.py
@@ -25,11 +25,6 @@
 def ring_route(axis, steps):
     count = lax.axis_size(axis)
     return [(source, (source + steps) % count) for source in range(count)]
-
-
-def line_route(axis, distance):
-    devices = range(lax.axis_size(axis))
-    return [(i - distance, i) for i in devices if i - distance in devices]
 
 
 def iota(shape, axis):
@@ -285,6 +280,7 @@
         rows_x[pl.ds(first, LANES), :] = dot_nt(unit, tiled)
 
     many = 8
+    at_last = lax.axis_index("py") == lax.axis_size("py") - 1
 
     def build_own(c, carry):
         for u in range(many):
@@ -301,7 +297,7 @@
                 pl.multiple_of(owned_len + first, LANES),
             )
             put_rows(
-                high_y_ref[:, pl.ds(first, LANES)],
+                jnp.where(at_last, 0.0, high_y_ref[:, pl.ds(first, LANES)]),
                 pl.multiple_of(owned_len + face_len + first, LANES),
             )
         return carry
@@ -586,7 +582,7 @@
     low_x = own_rows[:, interior : interior + face_len]
     low_y = own_rows[:, interior + face_len :]
     high_x = lax.ppermute(low_x, "px", ring_route("px", -1))
-    high_y = lax.ppermute(low_y, "py", line_route("py", -1))
+    high_y = lax.ppermute(low_y, "py", ring_route("py", -1))
     live = elem_count[0]
     smem = pl.BlockSpec(memory_space=pltpu.SMEM)
     vmem = pl.BlockSpec(memory_space=pltpu.VMEM)

time: 62.8 us -> 63.2 us (level)
    all_to_all x1, starting transfers between devices: 4.79 us -> 7.03 us  [on_device(): gathered = lax.all_to_all(gram, ('px', 'py'), 0, 0)]
    ppermute x1, starting transfers between devices: 2.08 us -> 0.22 us  [on_device(): high_y = lax.ppermute(low_y, 'py', ring_route('py', -1))]
where the time goes in v4:
time: 63.2 us; the launch traced here: 62.8 us
  Pallas kernels  49.5 us (78%)
  starting transfers between devices  11 us (17%)
  between operations  1.35 us (2%)
  local copies, waits for them, and re-layouts  0.99 us (2%)
    pallas_call x1, Pallas kernels, on_device(): pl.pallas_call(functools.partial(term_kernel, width, nloc), out_shape=(pl...  26.9 us
    pallas_call x1, Pallas kernels, on_device(): pl.pallas_call(functools.partial(add_kernel, width, nloc, interior), out_...  17.5 us
    all_to_all x1, starting transfers between devices, on_device(): gathered = lax.all_to_all(gram, ('px', 'py'), 0, 0)  7.03 us
    pallas_call x1, Pallas kernels, on_device(): pl.pallas_call(functools.partial(prepare_kernel, owned_len, face_len, wid...  3.65 us
    ppermute x1, starting transfers between devices, on_device(): back_x = lax.ppermute(side_x, 'px', ring_route('px', 1))  1.52 us
    pallas_call x1, Pallas kernels, on_device(): pl.pallas_call(functools.partial(finish_kernel, width, 1.0 / float(device...  1.46 us
  transfers between devices with their start and end apart: 5, of which 0 were waited for; matrix products, arithmetic and copies ran while one was open for 0% of the time, Pallas kernels for 34%

profile of v4, /device:TPU:19, one launch (start us, length us, event | category | flops | bytes accessed | tf_op | source)
XLA Modules:
  0.0 62.8 jit_solution(11682271115531047421)
XLA Ops:
  0.6 1.0 %fusion = (f32[16,2048]{1,0:T(8,128)S(1)}, f32[16,2048]{1,0:T(8,128)S(1)}) fusion(f32[16,8192]{1,0:T(8,128)} %bitcast.17), kind=kLoop, calls=%fused_computation | loop fusion | bytes 524288 | tf_op jit(solution)/shard_map/slice | solution.py:583
  1.6 0.2 collective-permute-start.1
  1.8 1.0 %collective-permute-start = (f32[16,2048]{1,0:T(8,128)S(1)}, f32[16,2048]{1,0:T(8,128)S(1)}, u32[]{:S(2)}, u32[]{:S(2)}) collective-permute-start(f32[16,2048]{1,0:T(8,128)S(1)} %get-tuple-element.36), channel_id=1, source_target_pairs={{0,28},{4,0},{8,4},{12,8},{16,12},{20,16},{24,20},{28,24},{1,29},{... | collective-permute-start | bytes 393224 | tf_op jit(solution)/shard_map/ppermute | solution.py:584
  3.5 3.6 %prepare.1 = (s32[22,1,1024]{2,1,0:T(1,128)}, s32[22,1,1024]{2,1,0:T(1,128)}, s32[24,128]{1,0:T(8,128)}, f32[256,128]{1,0:T(8,128)}, f32[16,128]{1,0:T(8,128)}, /*index=5*/f32[400,8,128]{2,1,0:T(8,128)}) custom-call(s32[1]{0:T(128)} %bitcast.14.count_ref, s32[2]{0:T(128)} %bloch_ref.1, f32[20,20]{1,0:T(8,128)} %stiff_elem_ref.1, f32[20,20]{1,0:T(8,128)} %mass_elem_ref.1, ...), custom_call_target="tpu_custom_call" | custom-call | tf_op jit(solution)/shard_map/prepare/pallas_call | solution.py:597
  7.1 0.0 collective-permute-done.1.high_y_ref
  7.1 0.0 collective-permute-done.high_x_ref
  7.1 26.9 %terms.1 = (f32[5120,128]{1,0:T(8,128)}, f32[32,2048]{1,0:T(8,128)S(1)}, f32[32,2048]{1,0:T(8,128)S(1)}, f32[32,8,128]{2,1,0:T(8,128)}) custom-call(s32[1]{0:T(128)} %bitcast.15.count_ref, s32[22528]{0:T(1024)} %bitcast.21, s32[3072]{0:T(1024)} %bitcast.23, f32[16,128]{1,0:T(8,128)} %get-tuple-element.22.turn_hbm, f32[16,8192]{1,0:T(8,128)} %bitcast.18, ...), custom_call_target="tpu_custom_call" | custom-call | tf_op jit(solution)/shard_map/terms/pallas_call | solution.py:632
  34.0 7.0 %all-to-all-start = ((f32[32,8,128]{2,1,0:T(8,128)}), f32[32,8,128]{2,1,0:T(8,128)S(1)}, u32[]{:S(2)}, u32[]{:S(2)}) async-start(f32[32,8,128]{2,1,0:T(8,128)} %get-tuple-element.31), calls=%async_computation | async-start | bytes 262144 | tf_op jit(solution)/shard_map/all_to_all | solution.py:663
  41.1 1.5 %collective-permute-start.2 = (f32[32,2048]{1,0:T(8,128)S(1)}, f32[32,2048]{1,0:T(8,128)S(1)}, u32[]{:S(2)}, u32[]{:S(2)}) collective-permute-start(f32[32,2048]{1,0:T(8,128)S(1)} %get-tuple-element.29), channel_id=1, source_target_pairs={{0,4},{4,8},{8,12},{12,16},{16,20},{20,24},{24,28},{28,0},{1,5},{5... | collective-permute-start | bytes 786440 | tf_op jit(solution)/shard_map/ppermute | solution.py:661
  42.6 1.2 %collective-permute-start.3 = (f32[32,2048]{1,0:T(8,128)S(1)}, f32[32,2048]{1,0:T(8,128)S(1)}, u32[]{:S(2)}, u32[]{:S(2)}) collective-permute-start(f32[32,2048]{1,0:T(8,128)S(1)} %get-tuple-element.30), channel_id=1, source_target_pairs={{0,1},{1,2},{2,3},{3,0},{4,5},{5,6},{6,7},{7,4},{8,9},{9,10},{10,1... | collective-permute-start | bytes 786440 | tf_op jit(solution)/shard_map/ppermute | solution.py:662
  43.9 17.5 %adds.1 = (f32[16,8192]{1,0:T(8,128)}, f32[16,8192]{1,0:T(8,128)}, f32[2,16,4096]{2,1,0:T(8,128)S(1)}) custom-call(s32[1]{0:T(128)} %bitcast.16.count_ref, s32[22528]{0:T(1024)} %bitcast.27, f32[5120,128]{1,0:T(8,128)} %get-tuple-element.25.term_hbm), custom_call_target="tpu_custom_call" | custom-call | flops 42949672960 | bytes 41943040 | tf_op jit(solution)/shard_map/adds/pallas_call | solution.py:665
  61.3 0.0 all-to-all-done.gram_ref
  61.4 0.0 collective-permute-done.2.back_x_ref
  61.4 0.0 collective-permute-done.3.back_y_ref
  61.4 1.5 %finish.1 = (f32[16,8192]{1,0:T(8,128)}, f32[16,8192]{1,0:T(8,128)}, f32[32,8]{1,0:T(8,128)}) custom-call(f32[16,8192]{1,0:T(8,128)} %get-tuple-element.26.curl_in, f32[16,8192]{1,0:T(8,128)} %get-tuple-element.27.mass_in, f32[2,16,4096]{2,1,0:T(8,128)S(1)} %get-tuple-element.28.face_ref, ...), custom_call_target="tpu_custom_call", output_to_operand_aliasing={{0}: (0, {}), {1}: (1, {})} | custom-call | tf_op jit(solution)/shard_map/finish/pallas_call | solution.py:690
Async XLA Ops:
  1.6 5.5 %collective-permute-start.1 = (f32[16,2048]{1,0:T(8,128)S(1)}, f32[16,2048]{1,0:T(8,128)S(1)}, u32[]{:S(2)}, u32[]{:S(2)}) collective-permute-start(f32[16,2048]{1,0:T(8,128)S(1)} %get-tuple-element.35), channel_id=1, source_target_pairs={{0,3},{1,0},{2,1},{3,2},{4,7},{5,4},{6,5},{7,6},{8,11},{9,8},{10,9... | collective-permute-start | bytes 393224 | tf_op jit(solution)/shard_map/ppermute | solution.py:585
  1.8 5.3 %collective-permute-start = (f32[16,2048]{1,0:T(8,128)S(1)}, f32[16,2048]{1,0:T(8,128)S(1)}, u32[]{:S(2)}, u32[]{:S(2)}) collective-permute-start(f32[16,2048]{1,0:T(8,128)S(1)} %get-tuple-element.36), channel_id=1, source_target_pairs={{0,28},{4,0},{8,4},{12,8},{16,12},{20,16},{24,20},{28,24},{1,29},{... | collective-permute-start | bytes 393224 | tf_op jit(solution)/shard_map/ppermute | solution.py:584
  34.0 27.3 %all-to-all-start = ((f32[32,8,128]{2,1,0:T(8,128)}), f32[32,8,128]{2,1,0:T(8,128)S(1)}, u32[]{:S(2)}, u32[]{:S(2)}) async-start(f32[32,8,128]{2,1,0:T(8,128)} %get-tuple-element.31), calls=%async_computation | async-start | bytes 262144 | tf_op jit(solution)/shard_map/all_to_all | solution.py:663
  41.1 20.3 %collective-permute-start.2 = (f32[32,2048]{1,0:T(8,128)S(1)}, f32[32,2048]{1,0:T(8,128)S(1)}, u32[]{:S(2)}, u32[]{:S(2)}) collective-permute-start(f32[32,2048]{1,0:T(8,128)S(1)} %get-tuple-element.29), channel_id=1, source_target_pairs={{0,4},{4,8},{8,12},{12,16},{16,20},{20,24},{24,28},{28,0},{1,5},{5... | collective-permute-start | bytes 786440 | tf_op jit(solution)/shard_map/ppermute | solution.py:661
  42.6 18.8 %collective-permute-start.3 = (f32[32,2048]{1,0:T(8,128)S(1)}, f32[32,2048]{1,0:T(8,128)S(1)}, u32[]{:S(2)}, u32[]{:S(2)}) collective-permute-start(f32[32,2048]{1,0:T(8,128)S(1)} %get-tuple-element.30), channel_id=1, source_target_pairs={{0,1},{1,2},{2,3},{3,0},{4,5},{5,6},{6,7},{7,4},{8,9},{9,10},{10,1... | collective-permute-start | bytes 786440 | tf_op jit(solution)/shard_map/ppermute | solution.py:662

commit v5 on v4

--- a/solution.py
+++ b/solution.py
@@ -63,11 +63,11 @@
     at_end = lax.axis_index("px") == lax.axis_size("px") - 1
     live = count_ref[0]
 
-    curl_lane = iota((8, LANES), 1) // width % 2 == 0
+    curl_lane = iota((1, LANES), 1) // width % 2 == 0
 
     def build_coef(j, carry):
         for i in range(nloc):
-            coef_ref[j * nloc + i] = jnp.where(curl_lane, stiff_elem_ref[j, i], mass_elem_ref[j, i])
+            coef_ref[pl.ds(j * nloc + i, 1), :] = jnp.where(curl_lane, stiff_elem_ref[j, i], mass_elem_ref[j, i])
         return carry
 
     lax.fori_loop(0, nloc, build_coef, 0)
@@ -344,7 +344,9 @@
                     gath[pl.ds(pl.multiple_of(there + i * BLOCK_ROWS + h, 8), 8), :] for h in halves
                 ]
                 for q in range(part):
-                    coef = coef_ref[(t * part + q) * nloc + i]
+                    coef = jnp.broadcast_to(
+                        coef_ref[pl.ds((t * part + q) * nloc + i, 1), :], (8, LANES)
+                    )
                     for n, value in enumerate(values):
                         product = coef * value
                         totals[q][n] = product if i == 0 else totals[q][n] + product
@@ -399,11 +401,15 @@
         at = pl.ds(pl.multiple_of(c * deep, BLOCK_ROWS), deep)
         left, left_low = split(gath[at, :])
         right, right_low = split(term_ref[at, :])
-        gram_acc[...] += lax.dot_general(
-            jnp.concatenate([left, left, left_low], axis=0),
-            jnp.concatenate([right, right_low, right], axis=0),
-            (((0,), (0,)), ((), ())),
+        over_rows = (((0,), (0,)), ((), ()))
+        gram_acc[:, : 2 * LANES] += lax.dot_general(
+            left,
+            jnp.concatenate([right, right_low], axis=1),
+            over_rows,
             preferred_element_type=F32,
+        )
+        gram_acc[:, 2 * LANES :] += lax.dot_general(
+            left_low, right, over_rows, preferred_element_type=F32
         )
         return carry
 
@@ -428,7 +434,7 @@
 
     lax.fori_loop(0, face_len // (4 * wide), fold_face, 0)
 
-    whole = gram_acc[...]
+    whole = gram_acc[:, :LANES] + gram_acc[:, LANES : 2 * LANES] + gram_acc[:, 2 * LANES :]
     total = whole[:width]
     for k in range(1, groups):
         part = whole[2 * width * k : 2 * width * k + width]
@@ -602,12 +608,12 @@
             jax.ShapeDtypeStruct((-(-nloc // 8) * 8, face_slots), jnp.int32),
             jax.ShapeDtypeStruct((capacity // groups, LANES), F32),
             jax.ShapeDtypeStruct((16, LANES), F32),
-            jax.ShapeDtypeStruct((nloc * nloc, 8, LANES), F32),
+            jax.ShapeDtypeStruct((nloc * nloc, LANES), F32),
         ),
         in_specs=[smem] * 4 + [vmem] * 4,
         out_specs=[vmem] * 5 + [left],
         scratch_shapes=[
-            pltpu.VMEM((nloc * nloc, 8, LANES), F32),
+            pltpu.VMEM((nloc * nloc, LANES), F32),
             pltpu.SemaphoreType.DMA,
         ],
         compiler_params=params,
@@ -649,7 +655,7 @@
             pltpu.VMEM((term_rows, LANES), F32),
             pltpu.VMEM((extent, LANES), F32),
             pltpu.VMEM((term_rows, LANES), F32),
-            pltpu.VMEM((LANES, LANES), F32),
+            pltpu.VMEM((LANES, 3 * LANES), F32),
             pltpu.SemaphoreType.DMA((6,)),
             pltpu.SemaphoreType.DMA((blocks,)),
         ]

time: 63.2 us -> 61.8 us (0.978)
  Pallas kernels: 49.5 us -> 47.7 us
    pallas_call x1, Pallas kernels: 26.9 us -> 25.6 us  [on_device(): pl.pallas_call(functools.partial(term_kernel, width, nloc), out_shape=(pl...]
  transfers between devices with their start and end apart: 5 -> 5, of which waited for: 0 -> 1; matrix products, arithmetic and copies ran while one was open for 0% -> 0% of each run, Pallas kernels for 34% -> 34%
where the time goes in v5:
time: 61.8 us; the launch traced here: 61.5 us
  Pallas kernels  47.7 us (77%)
  starting transfers between devices  11 us (18%)
  between operations  1.35 us (2%)
  local copies, waits for them, and re-layouts  0.99 us (2%)
    pallas_call x1, Pallas kernels, on_device(): pl.pallas_call(functools.partial(term_kernel, width, nloc), out_shape=(pl...  25.6 us
    pallas_call x1, Pallas kernels, on_device(): pl.pallas_call(functools.partial(add_kernel, width, nloc, interior), out_...  17.5 us
    all_to_all x1, starting transfers between devices, on_device(): gathered = lax.all_to_all(gram, ('px', 'py'), 0, 0)  7.01 us
    pallas_call x1, Pallas kernels, on_device(): pl.pallas_call(functools.partial(prepare_kernel, owned_len, face_len, wid...  3.14 us
    ppermute x1, starting transfers between devices, on_device(): back_x = lax.ppermute(side_x, 'px', ring_route('px', 1))  1.52 us
    pallas_call x1, Pallas kernels, on_device(): pl.pallas_call(functools.partial(finish_kernel, width, 1.0 / float(device...  1.46 us
    ppermute x1, starting transfers between devices, on_device(): back_y = lax.ppermute(side_y, 'py', ring_route('py', 1))  1.25 us
  transfers between devices with their start and end apart: 5, of which 1 were waited for; matrix products, arithmetic and copies ran while one was open for 0% of the time, Pallas kernels for 34%

profile of v5, /device:TPU:19, one launch (start us, length us, event | category | flops | bytes accessed | tf_op | source)
XLA Modules:
  0.0 61.5 jit_solution(14746846752307958420)
XLA Ops:
  0.6 1.0 %fusion = (f32[16,2048]{1,0:T(8,128)S(1)}, f32[16,2048]{1,0:T(8,128)S(1)}) fusion(f32[16,8192]{1,0:T(8,128)} %bitcast.17), kind=kLoop, calls=%fused_computation | loop fusion | bytes 524288 | tf_op jit(solution)/shard_map/slice | solution.py:589
  1.6 0.2 collective-permute-start.1
  1.8 1.0 %collective-permute-start = (f32[16,2048]{1,0:T(8,128)S(1)}, f32[16,2048]{1,0:T(8,128)S(1)}, u32[]{:S(2)}, u32[]{:S(2)}) collective-permute-start(f32[16,2048]{1,0:T(8,128)S(1)} %get-tuple-element.36), channel_id=1, source_target_pairs={{0,28},{4,0},{8,4},{12,8},{16,12},{20,16},{24,20},{28,24},{1,29},{... | collective-permute-start | bytes 393224 | tf_op jit(solution)/shard_map/ppermute | solution.py:590
  3.5 3.1 %prepare.1 = (s32[22,1,1024]{2,1,0:T(1,128)}, s32[22,1,1024]{2,1,0:T(1,128)}, s32[24,128]{1,0:T(8,128)}, f32[256,128]{1,0:T(8,128)}, f32[16,128]{1,0:T(8,128)}, /*index=5*/f32[400,128]{1,0:T(8,128)}) custom-call(s32[1]{0:T(128)} %bitcast.14.count_ref, s32[2]{0:T(128)} %bloch_ref.1, f32[20,20]{1,0:T(8,128)} %stiff_elem_ref.1, f32[20,20]{1,0:T(8,128)} %mass_elem_ref.1, ...), custom_call_target="tpu_custom_call" | custom-call | tf_op jit(solution)/shard_map/prepare/pallas_call | solution.py:603
  6.6 0.0 collective-permute-done.1.high_y_ref
  6.6 0.5 collective-permute-done.high_x_ref
  7.1 25.6 %terms.1 = (f32[5120,128]{1,0:T(8,128)}, f32[32,2048]{1,0:T(8,128)S(1)}, f32[32,2048]{1,0:T(8,128)S(1)}, f32[32,8,128]{2,1,0:T(8,128)}) custom-call(s32[1]{0:T(128)} %bitcast.15.count_ref, s32[22528]{0:T(1024)} %bitcast.21, s32[3072]{0:T(1024)} %bitcast.23, f32[16,128]{1,0:T(8,128)} %get-tuple-element.22.turn_hbm, f32[16,8192]{1,0:T(8,128)} %bitcast.18, ...), custom_call_target="tpu_custom_call" | custom-call | tf_op jit(solution)/shard_map/terms/pallas_call | solution.py:638
  32.8 7.0 %all-to-all-start = ((f32[32,8,128]{2,1,0:T(8,128)}), f32[32,8,128]{2,1,0:T(8,128)S(1)}, u32[]{:S(2)}, u32[]{:S(2)}) async-start(f32[32,8,128]{2,1,0:T(8,128)} %get-tuple-element.31), calls=%async_computation | async-start | bytes 262144 | tf_op jit(solution)/shard_map/all_to_all | solution.py:669
  39.8 1.5 %collective-permute-start.2 = (f32[32,2048]{1,0:T(8,128)S(1)}, f32[32,2048]{1,0:T(8,128)S(1)}, u32[]{:S(2)}, u32[]{:S(2)}) collective-permute-start(f32[32,2048]{1,0:T(8,128)S(1)} %get-tuple-element.29), channel_id=1, source_target_pairs={{0,4},{4,8},{8,12},{12,16},{16,20},{20,24},{24,28},{28,0},{1,5},{5... | collective-permute-start | bytes 786440 | tf_op jit(solution)/shard_map/ppermute | solution.py:667
  41.3 1.2 %collective-permute-start.3 = (f32[32,2048]{1,0:T(8,128)S(1)}, f32[32,2048]{1,0:T(8,128)S(1)}, u32[]{:S(2)}, u32[]{:S(2)}) collective-permute-start(f32[32,2048]{1,0:T(8,128)S(1)} %get-tuple-element.30), channel_id=1, source_target_pairs={{0,1},{1,2},{2,3},{3,0},{4,5},{5,6},{6,7},{7,4},{8,9},{9,10},{10,1... | collective-permute-start | bytes 786440 | tf_op jit(solution)/shard_map/ppermute | solution.py:668
  42.5 17.5 %adds.1 = (f32[16,8192]{1,0:T(8,128)}, f32[16,8192]{1,0:T(8,128)}, f32[2,16,4096]{2,1,0:T(8,128)S(1)}) custom-call(s32[1]{0:T(128)} %bitcast.16.count_ref, s32[22528]{0:T(1024)} %bitcast.27, f32[5120,128]{1,0:T(8,128)} %get-tuple-element.25.term_hbm), custom_call_target="tpu_custom_call" | custom-call | flops 42949672960 | bytes 41943040 | tf_op jit(solution)/shard_map/adds/pallas_call | solution.py:671
  60.0 0.0 all-to-all-done.gram_ref
  60.0 0.0 collective-permute-done.2.back_x_ref
  60.1 0.0 collective-permute-done.3.back_y_ref
  60.1 1.5 %finish.1 = (f32[16,8192]{1,0:T(8,128)}, f32[16,8192]{1,0:T(8,128)}, f32[32,8]{1,0:T(8,128)}) custom-call(f32[16,8192]{1,0:T(8,128)} %get-tuple-element.26.curl_in, f32[16,8192]{1,0:T(8,128)} %get-tuple-element.27.mass_in, f32[2,16,4096]{2,1,0:T(8,128)S(1)} %get-tuple-element.28.face_ref, ...), custom_call_target="tpu_custom_call", output_to_operand_aliasing={{0}: (0, {}), {1}: (1, {})} | custom-call | tf_op jit(solution)/shard_map/finish/pallas_call | solution.py:696
Async XLA Ops:
  1.6 5.0 %collective-permute-start.1 = (f32[16,2048]{1,0:T(8,128)S(1)}, f32[16,2048]{1,0:T(8,128)S(1)}, u32[]{:S(2)}, u32[]{:S(2)}) collective-permute-start(f32[16,2048]{1,0:T(8,128)S(1)} %get-tuple-element.35), channel_id=1, source_target_pairs={{0,3},{1,0},{2,1},{3,2},{4,7},{5,4},{6,5},{7,6},{8,11},{9,8},{10,9... | collective-permute-start | bytes 393224 | tf_op jit(solution)/shard_map/ppermute | solution.py:591
  1.8 5.3 %collective-permute-start = (f32[16,2048]{1,0:T(8,128)S(1)}, f32[16,2048]{1,0:T(8,128)S(1)}, u32[]{:S(2)}, u32[]{:S(2)}) collective-permute-start(f32[16,2048]{1,0:T(8,128)S(1)} %get-tuple-element.36), channel_id=1, source_target_pairs={{0,28},{4,0},{8,4},{12,8},{16,12},{20,16},{24,20},{28,24},{1,29},{... | collective-permute-start | bytes 393224 | tf_op jit(solution)/shard_map/ppermute | solution.py:590
  32.8 27.3 %all-to-all-start = ((f32[32,8,128]{2,1,0:T(8,128)}), f32[32,8,128]{2,1,0:T(8,128)S(1)}, u32[]{:S(2)}, u32[]{:S(2)}) async-start(f32[32,8,128]{2,1,0:T(8,128)} %get-tuple-element.31), calls=%async_computation | async-start | bytes 262144 | tf_op jit(solution)/shard_map/all_to_all | solution.py:669
  39.8 20.3 %collective-permute-start.2 = (f32[32,2048]{1,0:T(8,128)S(1)}, f32[32,2048]{1,0:T(8,128)S(1)}, u32[]{:S(2)}, u32[]{:S(2)}) collective-permute-start(f32[32,2048]{1,0:T(8,128)S(1)} %get-tuple-element.29), channel_id=1, source_target_pairs={{0,4},{4,8},{8,12},{12,16},{16,20},{20,24},{24,28},{28,0},{1,5},{5... | collective-permute-start | bytes 786440 | tf_op jit(solution)/shard_map/ppermute | solution.py:667
  41.3 18.8 %collective-permute-start.3 = (f32[32,2048]{1,0:T(8,128)S(1)}, f32[32,2048]{1,0:T(8,128)S(1)}, u32[]{:S(2)}, u32[]{:S(2)}) collective-permute-start(f32[32,2048]{1,0:T(8,128)S(1)} %get-tuple-element.30), channel_id=1, source_target_pairs={{0,1},{1,2},{2,3},{3,0},{4,5},{5,6},{6,7},{7,4},{8,9},{9,10},{10,1... | collective-permute-start | bytes 786440 | tf_op jit(solution)/shard_map/ppermute | solution.py:668

commit v6 on v5

--- a/solution.py
+++ b/solution.py
@@ -61,7 +61,7 @@
     face_slots = face_table_ref.shape[1]
     groups = LANES // (2 * width)
     at_end = lax.axis_index("px") == lax.axis_size("px") - 1
-    live = count_ref[0]
+    live = count_ref[0, 0]
 
     curl_lane = iota((1, LANES), 1) // width % 2 == 0
 
@@ -367,7 +367,7 @@
         add_block(term_ref, accs, face_index_of, index_of, b, nloc, groups)
         return carry
 
-    live = count_ref[0]
+    live = count_ref[0, 0]
     blocks = (live + block_elems - 1) // block_elems
     face_blocks = jnp.minimum(blocks, face_slots // block_elems)
 
@@ -467,7 +467,7 @@
     block_terms = nloc * BLOCK_ROWS
     load = pltpu.make_async_copy(table_hbm, dofs_ref, sem)
     load.start()
-    live = count_ref[0]
+    live = count_ref[0, 0]
     blocks = (live + block_elems - 1) // block_elems
 
     def fetch(b):
@@ -589,7 +589,7 @@
     low_y = own_rows[:, interior + face_len :]
     high_x = lax.ppermute(low_x, "px", ring_route("px", -1))
     high_y = lax.ppermute(low_y, "py", ring_route("py", -1))
-    live = elem_count[0]
+    live = elem_count
     smem = pl.BlockSpec(memory_space=pltpu.SMEM)
     vmem = pl.BlockSpec(memory_space=pltpu.VMEM)
     left = pl.BlockSpec(memory_space=pl.ANY)

time: 61.8 us -> 61.8 us (level)
  no operation moved by 1% of the time
where the time goes in v6:
time: 61.8 us; the launch traced here: 61.5 us
  Pallas kernels  47.7 us (77%)
  starting transfers between devices  11 us (18%)
  between operations  1.35 us (2%)
  local copies, waits for them, and re-layouts  0.99 us (2%)
    pallas_call x1, Pallas kernels, on_device(): pl.pallas_call(functools.partial(term_kernel, width, nloc), out_shape=(pl...  25.6 us
    pallas_call x1, Pallas kernels, on_device(): pl.pallas_call(functools.partial(add_kernel, width, nloc, interior), out_...  17.5 us
    all_to_all x1, starting transfers between devices, on_device(): gathered = lax.all_to_all(gram, ('px', 'py'), 0, 0)  7.01 us
    pallas_call x1, Pallas kernels, on_device(): pl.pallas_call(functools.partial(prepare_kernel, owned_len, face_len, wid...  3.14 us
    ppermute x1, starting transfers between devices, on_device(): back_x = lax.ppermute(side_x, 'px', ring_route('px', 1))  1.52 us
    pallas_call x1, Pallas kernels, on_device(): pl.pallas_call(functools.partial(finish_kernel, width, 1.0 / float(device...  1.46 us
    ppermute x1, starting transfers between devices, on_device(): back_y = lax.ppermute(side_y, 'py', ring_route('py', 1))  1.25 us
  transfers between devices with their start and end apart: 5, of which 1 were waited for; matrix products, arithmetic and copies ran while one was open for 0% of the time, Pallas kernels for 34%

profile of v6, /device:TPU:19, one launch (start us, length us, event | category | flops | bytes accessed | tf_op | source)
XLA Modules:
  0.0 61.5 jit_solution(7854699776781301341)
XLA Ops:
  0.6 1.0 %fusion = (f32[16,2048]{1,0:T(8,128)S(1)}, f32[16,2048]{1,0:T(8,128)S(1)}) fusion(f32[16,8192]{1,0:T(8,128)} %bitcast.13), kind=kLoop, calls=%fused_computation | loop fusion | bytes 524288 | tf_op jit(solution)/shard_map/slice | solution.py:589
  1.6 0.2 collective-permute-start.1
  1.8 1.0 %collective-permute-start = (f32[16,2048]{1,0:T(8,128)S(1)}, f32[16,2048]{1,0:T(8,128)S(1)}, u32[]{:S(2)}, u32[]{:S(2)}) collective-permute-start(f32[16,2048]{1,0:T(8,128)S(1)} %get-tuple-element.36), channel_id=1, source_target_pairs={{0,28},{4,0},{8,4},{12,8},{16,12},{20,16},{24,20},{28,24},{1,29},{... | collective-permute-start | bytes 393224 | tf_op jit(solution)/shard_map/ppermute | solution.py:590
  3.5 3.1 %prepare.1 = (s32[22,1,1024]{2,1,0:T(1,128)}, s32[22,1,1024]{2,1,0:T(1,128)}, s32[24,128]{1,0:T(8,128)}, f32[256,128]{1,0:T(8,128)}, f32[16,128]{1,0:T(8,128)}, /*index=5*/f32[400,128]{1,0:T(8,128)}) custom-call(s32[1,1]{1,0:T(1,128)S(6)} %copy.16.count_ref, s32[2]{0:T(128)} %bloch_ref.1, f32[20,20]{1,0:T(8,128)} %stiff_elem_ref.1, f32[20,20]{1,0:T(8,128)} %mass_elem_ref.1, ...), custom_call_target="tpu_custom_call" | custom-call | tf_op jit(solution)/shard_map/prepare/pallas_call | solution.py:603
  6.6 0.0 collective-permute-done.1.high_y_ref
  6.6 0.5 collective-permute-done.high_x_ref
  7.1 25.6 %terms.1 = (f32[5120,128]{1,0:T(8,128)}, f32[32,2048]{1,0:T(8,128)S(1)}, f32[32,2048]{1,0:T(8,128)S(1)}, f32[32,8,128]{2,1,0:T(8,128)}) custom-call(s32[1,1]{1,0:T(1,128)S(6)} %copy.16.count_ref, s32[22528]{0:T(1024)} %bitcast.17, s32[3072]{0:T(1024)} %bitcast.19, f32[16,128]{1,0:T(8,128)} %get-tuple-element.22.turn_hbm, f32[16,8192]{1,0:T(8,128)} %bitcast.14, ...), custom_call_target="tpu_custom_call" | custom-call | tf_op jit(solution)/shard_map/terms/pallas_call | solution.py:638
  32.8 7.0 %all-to-all-start = ((f32[32,8,128]{2,1,0:T(8,128)}), f32[32,8,128]{2,1,0:T(8,128)S(1)}, u32[]{:S(2)}, u32[]{:S(2)}) async-start(f32[32,8,128]{2,1,0:T(8,128)} %get-tuple-element.31), calls=%async_computation | async-start | bytes 262144 | tf_op jit(solution)/shard_map/all_to_all | solution.py:669
  39.8 1.5 %collective-permute-start.2 = (f32[32,2048]{1,0:T(8,128)S(1)}, f32[32,2048]{1,0:T(8,128)S(1)}, u32[]{:S(2)}, u32[]{:S(2)}) collective-permute-start(f32[32,2048]{1,0:T(8,128)S(1)} %get-tuple-element.29), channel_id=1, source_target_pairs={{0,4},{4,8},{8,12},{12,16},{16,20},{20,24},{24,28},{28,0},{1,5},{5... | collective-permute-start | bytes 786440 | tf_op jit(solution)/shard_map/ppermute | solution.py:667
  41.3 1.2 %collective-permute-start.3 = (f32[32,2048]{1,0:T(8,128)S(1)}, f32[32,2048]{1,0:T(8,128)S(1)}, u32[]{:S(2)}, u32[]{:S(2)}) collective-permute-start(f32[32,2048]{1,0:T(8,128)S(1)} %get-tuple-element.30), channel_id=1, source_target_pairs={{0,1},{1,2},{2,3},{3,0},{4,5},{5,6},{6,7},{7,4},{8,9},{9,10},{10,1... | collective-permute-start | bytes 786440 | tf_op jit(solution)/shard_map/ppermute | solution.py:668
  42.5 17.5 %adds.1 = (f32[16,8192]{1,0:T(8,128)}, f32[16,8192]{1,0:T(8,128)}, f32[2,16,4096]{2,1,0:T(8,128)S(1)}) custom-call(s32[1,1]{1,0:T(1,128)S(6)} %copy.16.count_ref, s32[22528]{0:T(1024)} %bitcast.23, f32[5120,128]{1,0:T(8,128)} %get-tuple-element.25.term_hbm), custom_call_target="tpu_custom_call" | custom-call | flops 42949672960 | bytes 41943040 | tf_op jit(solution)/shard_map/adds/pallas_call | solution.py:671
  60.0 0.0 all-to-all-done.gram_ref
  60.0 0.0 collective-permute-done.2.back_x_ref
  60.1 0.0 collective-permute-done.3.back_y_ref
  60.1 1.5 %finish.1 = (f32[16,8192]{1,0:T(8,128)}, f32[16,8192]{1,0:T(8,128)}, f32[32,8]{1,0:T(8,128)}) custom-call(f32[16,8192]{1,0:T(8,128)} %get-tuple-element.26.curl_in, f32[16,8192]{1,0:T(8,128)} %get-tuple-element.27.mass_in, f32[2,16,4096]{2,1,0:T(8,128)S(1)} %get-tuple-element.28.face_ref, ...), custom_call_target="tpu_custom_call", output_to_operand_aliasing={{0}: (0, {}), {1}: (1, {})} | custom-call | tf_op jit(solution)/shard_map/finish/pallas_call | solution.py:696
Async XLA Ops:
  1.6 5.0 %collective-permute-start.1 = (f32[16,2048]{1,0:T(8,128)S(1)}, f32[16,2048]{1,0:T(8,128)S(1)}, u32[]{:S(2)}, u32[]{:S(2)}) collective-permute-start(f32[16,2048]{1,0:T(8,128)S(1)} %get-tuple-element.35), channel_id=1, source_target_pairs={{0,3},{1,0},{2,1},{3,2},{4,7},{5,4},{6,5},{7,6},{8,11},{9,8},{10,9... | collective-permute-start | bytes 393224 | tf_op jit(solution)/shard_map/ppermute | solution.py:591
  1.8 5.3 %collective-permute-start = (f32[16,2048]{1,0:T(8,128)S(1)}, f32[16,2048]{1,0:T(8,128)S(1)}, u32[]{:S(2)}, u32[]{:S(2)}) collective-permute-start(f32[16,2048]{1,0:T(8,128)S(1)} %get-tuple-element.36), channel_id=1, source_target_pairs={{0,28},{4,0},{8,4},{12,8},{16,12},{20,16},{24,20},{28,24},{1,29},{... | collective-permute-start | bytes 393224 | tf_op jit(solution)/shard_map/ppermute | solution.py:590
  32.8 27.3 %all-to-all-start = ((f32[32,8,128]{2,1,0:T(8,128)}), f32[32,8,128]{2,1,0:T(8,128)S(1)}, u32[]{:S(2)}, u32[]{:S(2)}) async-start(f32[32,8,128]{2,1,0:T(8,128)} %get-tuple-element.31), calls=%async_computation | async-start | bytes 262144 | tf_op jit(solution)/shard_map/all_to_all | solution.py:669
  39.8 20.3 %collective-permute-start.2 = (f32[32,2048]{1,0:T(8,128)S(1)}, f32[32,2048]{1,0:T(8,128)S(1)}, u32[]{:S(2)}, u32[]{:S(2)}) collective-permute-start(f32[32,2048]{1,0:T(8,128)S(1)} %get-tuple-element.29), channel_id=1, source_target_pairs={{0,4},{4,8},{8,12},{12,16},{16,20},{20,24},{24,28},{28,0},{1,5},{5... | collective-permute-start | bytes 786440 | tf_op jit(solution)/shard_map/ppermute | solution.py:667
  41.3 18.8 %collective-permute-start.3 = (f32[32,2048]{1,0:T(8,128)S(1)}, f32[32,2048]{1,0:T(8,128)S(1)}, u32[]{:S(2)}, u32[]{:S(2)}) collective-permute-start(f32[32,2048]{1,0:T(8,128)S(1)} %get-tuple-element.30), channel_id=1, source_target_pairs={{0,1},{1,2},{2,3},{3,0},{4,5},{5,6},{6,7},{7,4},{8,9},{9,10},{10,1... | collective-permute-start | bytes 786440 | tf_op jit(solution)/shard_map/ppermute | solution.py:668
